TPU v7x, 32 devices: a whole 2x2x4 slice. The times are simulated.
32 devices in a mesh: dp: 4 (over x, core), mp: 8 (over z, y).
Axes of the slice: x: 2, y: 2, z: 4, core: 2. Of those that a mesh axis runs over, the one named last changes fastest.
Arguments:
- tokens: bfloat16 [16384, 1792], P(('dp', 'mp')), may hold values from -12 to 12
- first_norm_gain: float32 [1792], replicated, may hold values from 0.25 to 1.75
- query_weight: bfloat16 [1792, 896], replicated, may hold values from -0.144098955 to 0.144098955
- key_weight: bfloat16 [1792, 896], replicated, may hold values from -3.5670397 to 3.5670397
- value_weight: bfloat16 [1792, 896], replicated, may hold values from -0.125 to 0.125
- output_weight: bfloat16 [896, 1792], replicated, may hold values from -0.1875 to 0.1875
- lengths: int32 [256], P(('dp', 'mp')), may hold values from 1 to 64, as said below
- request_adapter: int32 [256], P(('dp', 'mp')), may hold values from 0 to 31, as said below
- slot_adapter_ids: int32 [32], replicated, may hold values from 0 to 31, as said below
- plugin_shrink_maps: bfloat16 [32, 1792, 32], P('mp'), may hold values from -0.125 to 0.125
- plugin_grow_maps: bfloat16 [32, 2, 16, 896], P('mp'), may hold values from -1.5 to 1.5
- device_token_order: int32 [32, 512], P(('dp', 'mp')), may hold values from 0 to 511, each once within a row
- second_norm_gain: float32 [1792], replicated, may hold values from 0.25 to 1.75
- gate_weight: bfloat16 [1792, 3584], P(('dp', 'mp')), may hold values from -0.125 to 0.125
- up_weight: bfloat16 [1792, 3584], P(('dp', 'mp')), may hold values from -0.125 to 0.125
Outputs:
- residual: bfloat16 [16384, 1792], P(('dp', 'mp'))
- hidden: bfloat16 [16384, 3584], P(('dp', 'mp'))
Inputs may be any that keep to these rules, and one draw needn't show every extreme that they name: `slot_adapter_ids`: a permutation of the adapter ids; slot s lives on index s // 4 of mp. `request_adapter`: the 8 requests of one device use adapters whose slots lie on distinct indices of mp. `lengths`: on every device some request has length 64.
All inputs are finite; a program needn't handle non-finite values.
Results may differ from a plain program's by a relative error of at most 0.011.
Values may be sent and summed in bfloat16 or wider, within the bound.
A program may use at most 192 MiB of HBM per device.

v0:
```python
import jax
import jax.numpy as jnp
from jax import lax
from jax.sharding import PartitionSpec as P

EMBED_SPAN = 1792
HEADS = 8
HD = 112
LATENT_BREADTH = 16
REQ_DEV = 8
SLOTR = 64
WINDOW = 32
SINKS = 4


PLUGIN_STRENGTH = 2.0
EPSILON = 1e-05


def normalize(rows_in, gain_vec):
    floated = rows_in.astype(jnp.float32)
    scale = lax.rsqrt(jnp.mean(floated * floated, axis=-1, keepdims=True) + EPSILON)
    return (floated * scale * gain_vec).astype(jnp.bfloat16)


def low_rank(request_rows, down_matrices, growth_coefficients):
    thin_latent_image = jnp.einsum(
        "std,sdk->stk", request_rows, down_matrices, preferred_element_type=jnp.float32
    ).astype(jnp.bfloat16)
    queries_lowrank_delta = (
        jnp.einsum(
            "stk,skh->sth",
            thin_latent_image[..., :LATENT_BREADTH],
            growth_coefficients[:, 0],
            preferred_element_type=jnp.float32,
        )
        * PLUGIN_STRENGTH
    )
    values_lowrank_delta = (
        jnp.einsum(
            "stk,skh->sth",
            thin_latent_image[..., LATENT_BREADTH:],
            growth_coefficients[:, 1],
            preferred_element_type=jnp.float32,
        )
        * PLUGIN_STRENGTH
    )
    return jnp.concatenate(
        [queries_lowrank_delta.astype(jnp.bfloat16), values_lowrank_delta.astype(jnp.bfloat16)],
        axis=-1,
    )


def attend(query, key, value, request_len):
    queries = query.reshape(REQ_DEV, SLOTR, HEADS, HD)
    head_keys = key.reshape(REQ_DEV, SLOTR, HEADS, HD)
    head_values = value.reshape(REQ_DEV, SLOTR, HEADS, HD)
    scores = jnp.einsum(
        "rqhd,rkhd->rhqk", queries, head_keys, preferred_element_type=jnp.float32
    ) * HD ** (-0.5)
    places = jnp.arange(SLOTR)
    query_place = places[:, None]
    key_place = places[None, :]
    allowed = (key_place <= query_place) & (
        (query_place - key_place < WINDOW) | (key_place < SINKS)
    )
    key_live = places[None, :] < request_len[:, None]
    visible_lookup_flags = allowed[None, None, :, :] & key_live[:, None, None, :]
    scores = jnp.where(visible_lookup_flags, scores, -1e30)
    row_max = jnp.max(scores, axis=-1, keepdims=True)
    expo = jnp.where(visible_lookup_flags, jnp.exp(scores - row_max), 0.0)
    softmax_w = (expo / jnp.sum(expo, axis=-1, keepdims=True)).astype(jnp.bfloat16)
    attended = jnp.einsum(
        "rhqk,rkhd->rqhd", softmax_w, head_values, preferred_element_type=jnp.float32
    ).astype(jnp.bfloat16)
    query_live = (places[None, :] < request_len[:, None])[:, :, None, None]
    attended = jnp.where(query_live, attended, jnp.zeros_like(attended))
    return attended.reshape(REQ_DEV * SLOTR, HEADS * HD)


def local(
    tokens,
    first_norm_gain,
    query_weight,
    key_weight,
    value_weight,
    output_weight,
    lengths,
    request_adapter,
    slot_adapter_ids,
    plugin_shrink_maps,
    plugin_grow_maps,
    device_token_order,
    second_norm_gain,
    gate_weight,
    up_weight,
):
    owner_count = lax.axis_size("mp")
    resident_slots = plugin_shrink_maps.shape[0]
    tok_dev = tokens.shape[0]
    hw_size = query_weight.shape[1]
    normed = normalize(tokens, first_norm_gain)
    matches = (slot_adapter_ids[None, :] == request_adapter[:, None]).astype(jnp.int32)
    slot_ids = jnp.sum(
        matches * jnp.arange(slot_adapter_ids.shape[0], dtype=jnp.int32)[None, :], axis=1
    )
    request_rows = normed.reshape(REQ_DEV, SLOTR, EMBED_SPAN)
    owner_index = slot_ids // resident_slots
    within = slot_ids % resident_slots
    routing = (jnp.arange(owner_count)[:, None] == owner_index[None, :]).astype(jnp.bfloat16)
    slot_pick = (jnp.arange(resident_slots)[None, :] == within[:, None]).astype(jnp.bfloat16)
    outgoing = jnp.einsum(
        "or,rsd->osd", routing, request_rows, preferred_element_type=jnp.float32
    ).astype(jnp.bfloat16)
    chosen = jnp.dot(routing, slot_pick, preferred_element_type=jnp.float32).astype(jnp.bfloat16)
    incoming, chosen_adapter = (
        lax.all_to_all(outgoing, "mp", split_axis=0, concat_axis=0, tiled=True),
        lax.all_to_all(chosen, "mp", split_axis=0, concat_axis=0, tiled=True),
    )
    down_sel = jnp.einsum(
        "ge,erz->grz", chosen_adapter, plugin_shrink_maps, preferred_element_type=jnp.float32
    ).astype(jnp.bfloat16)
    up_sel = jnp.einsum(
        "uz,zirn->uirn", chosen_adapter, plugin_grow_maps, preferred_element_type=jnp.float32
    ).astype(jnp.bfloat16)
    deltas = low_rank(incoming, down_sel, up_sel)
    returned_rows = lax.all_to_all(deltas, "mp", split_axis=0, concat_axis=0, tiled=True)
    own_delta = jnp.einsum(
        "or,osh->rsh", routing, returned_rows, preferred_element_type=jnp.float32
    ).astype(jnp.bfloat16)
    queries_lowrank_delta = own_delta[..., :hw_size].reshape(tok_dev, hw_size).astype(jnp.float32)
    values_lowrank_delta = own_delta[..., hw_size:].reshape(tok_dev, hw_size).astype(jnp.float32)
    query = (
        jnp.dot(normed, query_weight, preferred_element_type=jnp.float32) + queries_lowrank_delta
    ).astype(jnp.bfloat16)
    key = jnp.dot(normed, key_weight, preferred_element_type=jnp.float32).astype(jnp.bfloat16)
    value = (
        jnp.dot(normed, value_weight, preferred_element_type=jnp.float32) + values_lowrank_delta
    ).astype(jnp.bfloat16)
    attended = attend(query, key, value, lengths)
    residual = (
        tokens.astype(jnp.float32)
        + jnp.dot(attended, output_weight, preferred_element_type=jnp.float32)
    ).astype(jnp.bfloat16)
    shuffled = residual[device_token_order[0]]
    regrouped = lax.all_to_all(shuffled, ("dp", "mp"), split_axis=0, concat_axis=0, tiled=True)
    mlp_input = normalize(regrouped, second_norm_gain)
    full_gate, full_up = (
        lax.all_gather(gate_weight, ("dp", "mp"), axis=0, tiled=True),
        lax.all_gather(up_weight, ("dp", "mp"), axis=0, tiled=True),
    )
    gate = jnp.dot(mlp_input, full_gate, preferred_element_type=jnp.float32)
    upper = jnp.dot(mlp_input, full_up, preferred_element_type=jnp.float32)
    hidden = (jax.nn.silu(gate) * upper).astype(jnp.bfloat16)
    return (residual, hidden)


def solution(mesh):
    return jax.shard_map(
        local,
        mesh=mesh,
        in_specs=(
            P(("dp", "mp"), None),
            P(),
            P(),
            P(),
            P(),
            P(),
            P(("dp", "mp")),
            P(("dp", "mp")),
            P(),
            P("mp", None, None),
            P("mp", None, None, None),
            P(("dp", "mp"), None),
            P(),
            P(("dp", "mp"), None),
            P(("dp", "mp"), None),
        ),
        out_specs=(P(("dp", "mp"), None), P(("dp", "mp"), None)),
        check_vma=False,
    )
```

profile of v0, /device:TPU:0, one launch (start us, length us, event | category | flops | bytes accessed | tf_op | source)
XLA Modules:
  0.0 333.6 jit_solution(13671005667863518214)
XLA Ops:
  7.2 0.0 copy-start
  7.2 0.0 copy-start.8
  7.2 0.0 all-gather.3.cloned.1.call-start
  7.2 0.7 all-gather.3.cloned.1.call-update
  7.9 0.0 all-gather.5.cloned.1.call-start
  8.0 0.7 all-gather.5.cloned.1.call-update
  8.7 0.9 select_reduce_fusion
  9.5 0.3 fusion.14
  9.8 0.7 copy.70
  10.5 7.3 %all-to-all-start.1 = ((bf16[8,1,4]{2,1,0:T(2,128)(2,1)}), bf16[8,1,4]{2,1,0:T(2,128)(2,1)S(1)}, u32[]{:S(2)}, u32[]{:S(2)}) async-start(bf16[8,1,4]{2,1,0:T(2,128)(2,1)} %copy.70), calls=%async_computation.1 | async-start | bytes 8192 | tf_op jit(solution)/shard_map/all_to_all | solution.py:118
  17.8 2.1 fusion.1
  19.9 0.0 copy-done.8
  19.9 0.0 copy-done.2
  19.9 0.5 fusion.3
  20.4 0.0 copy-start.3
  20.4 1.2 copy-done.3
  21.6 1.3 convolution_convert_fusion.1
  22.9 1.5 copy.69
  24.5 0.0 all-to-all-done.1
  24.5 6.1 %all-to-all-start = ((bf16[8,64,1792]{2,1,0:T(8,128)(2,1)}), bf16[8,64,1792]{2,1,0:T(8,128)(2,1)}, u32[]{:S(2)}, u32[]{:S(2)}) async-start(bf16[8,64,1792]{2,1,0:T(8,128)(2,1)} %copy.69), calls=%async_computation | async-start | bytes 3670016 | tf_op jit(solution)/shard_map/all_to_all | solution.py:117
  30.6 0.1 copy.71
  30.7 0.3 convolution_convert_fusion.5
  31.0 0.7 slice_bitcast_fusion.1
  31.8 2.5 convolution_convert_fusion.2
  34.2 58.4 %all-to-all-done = bf16[8,64,1792]{2,1,0:T(8,128)(2,1)} async-done(((bf16[8,64,1792]{2,1,0:T(8,128)(2,1)}), bf16[8,64,1792]{2,1,0:T(8,128)(2,1)}, u32[]{:S(2)}, u32[]{:S(2)}) %all-to-all-start) | async-done | bytes 1835040 | tf_op jit(solution)/shard_map/all_to_all | solution.py:117
  92.6 2.4 convolution_convert_fusion.6
  95.0 0.0 copy-done.6
  95.0 0.4 multiply_convert_fusion.1
  95.4 0.4 multiply_convert_fusion.2
  95.9 1.4 pad_maximum_fusion
  97.3 4.5 %all-to-all-start.2 = ((bf16[8,64,1792]{2,1,0:T(8,128)(2,1)}), bf16[8,64,1792]{2,1,0:T(8,128)(2,1)}, u32[]{:S(2)}, u32[]{:S(2)}) async-start(bf16[8,64,1792]{2,1,0:T(8,128)(2,1)} %pad_maximum_fusion), calls=%async_computation.2 | async-start | bytes 3670016 | tf_op jit(solution)/shard_map/all_to_all | solution.py:127
  101.8 0.0 copy-start.10
  101.8 0.0 copy-start.12
  101.8 5.5 %convolution_convert_fusion.4 = bf16[512,896]{1,0:T(8,128)(2,1)} fusion(bf16[512,1792]{1,0:T(8,128)(2,1)} %copy-done.3, bf16[1792,896]{1,0:T(8,128)(2,1)} %param.18), kind=kOutput, calls=%fused_computation.31 | convolution fusion | flops 1644625920 | bytes 5963776 | tf_op jit(solution)/shard_map/dot_general | solution.py:136
  107.3 3.1 reshape.211
  110.5 0.1 iota_compare_fusion.4
  110.6 0.1 fusion.30
  110.7 0.1 broadcast_and_fusion
  110.8 61.7 %all-to-all-done.2 = bf16[8,64,1792]{2,1,0:T(8,128)(2,1)} async-done(((bf16[8,64,1792]{2,1,0:T(8,128)(2,1)}), bf16[8,64,1792]{2,1,0:T(8,128)(2,1)}, u32[]{:S(2)}, u32[]{:S(2)}) %all-to-all-start.2) | async-done | bytes 1835040 | tf_op jit(solution)/shard_map/all_to_all | solution.py:127
  172.5 2.8 convolution_convert_fusion
  175.3 0.0 copy-start.11
  175.3 1.5 slice_convert_fusion.1
  176.8 0.4 copy.79
  177.1 0.7 copy-done.11
  177.9 0.8 copy-done.4
  178.6 3.0 fusion.8
  181.7 3.1 reshape.210
  184.8 2.0 copy.78
  186.8 0.1 copy-done.5
  186.9 4.9 %fusion.9 = bf16[512,896]{1,0:T(8,128)(2,1)} fusion(f32[8,64,896]{2,1,0:T(8,128)S(1)} %copy.78, bf16[512,1792]{1,0:T(8,128)(2,1)S(1)} %copy-done.5, bf16[1792,896]{1,0:T(8,128)(2,1)} %param.19), kind=kOutput, calls=%fused_computation.25 | convolution fusion | flops 1645084672 | bytes 7798784 | tf_op jit(solution)/shard_map/dot_general | solution.py:138
  191.8 3.1 reshape.209
  194.9 4.1 %fusion.43 = (f32[8,8,64]{2,1,0:T(8,128)S(1)}, f32[8,8,64,64]{2,3,1,0:T(8,128)}) fusion(pred[8,64,64]{1,2,0:T(8,128)(4,1)S(1)} %broadcast_and_fusion, bf16[8,64,8,112]{3,2,1,0:T(8,128)(2,1)} %reshape.211, bf16[8,64,8,112]{3,2,1,0:T(8,128)(2,1)} %reshape.210), kind=kOutput, calls=%fused_computation.85 | convolution fusion | flops 60031040 | bytes 2932736 | tf_op jit(solution)/shard_map/sub | solution.py:71
  199.0 2.6 fusion.13
  201.6 1.7 copy.84
  203.3 2.7 reshape.212
  206.0 0.0 copy-done
  206.1 5.1 %fusion.4 = bf16[512,1792]{1,0:T(8,128)(2,1)} fusion(bf16[512,1792]{1,0:T(8,128)(2,1)} %param.15, bf16[512,896]{1,0:T(8,128)(2,1)} %reshape.212, bf16[896,1792]{1,0:T(8,128)(2,1)S(1)} %copy-done), kind=kOutput, calls=%fused_computation.9 | convolution fusion | flops 1646919680 | bytes 7798784 | tf_op jit(solution)/shard_map/dot_general | solution.py:143
  211.1 6.5 %gather_fusion = bf16[512,1792]{1,0:T(8,128)(2,1)} fusion(bf16[512,1792]{1,0:T(8,128)(2,1)} %fusion.4, s32[1024]{0:T(1024)S(1)} %pad_clamp_fusion), kind=kCustom, calls=%fused_computation | custom fusion | bytes 3672064 | tf_op jit(solution)/shard_map/gather | solution.py:145
  217.6 81.8 %all_to_all.31 = bf16[32,16,1792]{2,1,0:T(8,128)(2,1)S(1)} all-to-all(bf16[32,16,1792]{2,1,0:T(8,128)(2,1)} %bitcast.57), channel_id=1, replica_groups=mesh['dp'=4,'mp'=8] {'dp','mp'}, dimensions={0} | all-to-all | bytes 3670016 | tf_op jit(solution)/shard_map/all_to_all | solution.py:146
  299.4 0.4 multiply_reduce_fusion
  299.9 0.1 rsqrt.21
  300.0 1.7 fusion.6
  301.7 12.1 %fusion.52 = f32[512,3584]{1,0:T(8,128)} fusion(bf16[512,1792]{1,0:T(8,128)(2,1)} %fusion.6, bf16[1792,3584]{1,0:T(8,128)(2,1)} %all-gather.3.cloned.1.call-done), kind=kOutput, calls=%fused_computation.86 | convolution fusion | flops 6576668672 | bytes 22020096 | tf_op jit(solution)/shard_map/dot_general | solution.py:152
  313.8 13.0 %multiply_convert_fusion = bf16[512,3584]{1,0:T(8,128)(2,1)} fusion(f32[512,3584]{1,0:T(8,128)} %fusion.52, bf16[512,1792]{1,0:T(8,128)(2,1)} %fusion.6, bf16[1792,3584]{1,0:T(8,128)(2,1)} %all-gather.5.cloned.1.call-done), kind=kOutput, calls=%fused_computation.2 | convolution fusion | flops 6587678720 | bytes 25690112 | tf_op jit(solution)/shard_map/dot_general | solution.py:153
  (20 shorter events, 0.1 us)
Async XLA Ops:
  7.2 198.9 %copy-start = (bf16[896,1792]{1,0:T(8,128)(2,1)S(1)}, bf16[896,1792]{1,0:T(8,128)(2,1)}, u32[]{:S(2)}) copy-start(bf16[896,1792]{1,0:T(8,128)(2,1)} %param.20) | copy-start | bytes 9633796
  7.2 12.7 %copy-start.8 = (f32[1792]{0:T(1024)S(1)}, f32[1792]{0:T(1024)}, u32[]{:S(2)}) copy-start(f32[1792]{0:T(1024)} %param.16) | copy-start | bytes 21508
  7.2 294.5 %all-gather.3.cloned.1.call-start = ((), (), s32[]{:S(2)}) async-start(), calls=%async_computation.4 | async-start | bytes 13246464 | tf_op jit(solution)/shard_map/all_gather | solution.py:149
  7.9 305.9 %all-gather.5.cloned.1.call-start = ((), (), s32[]{:S(2)}) async-start(), calls=%async_computation.5 | async-start | bytes 13246464 | tf_op jit(solution)/shard_map/all_gather | solution.py:150
  10.5 14.0 %all-to-all-start.1 = ((bf16[8,1,4]{2,1,0:T(2,128)(2,1)}), bf16[8,1,4]{2,1,0:T(2,128)(2,1)S(1)}, u32[]{:S(2)}, u32[]{:S(2)}) async-start(bf16[8,1,4]{2,1,0:T(2,128)(2,1)} %copy.70), calls=%async_computation.1 | async-start | bytes 8192 | tf_op jit(solution)/shard_map/all_to_all | solution.py:118
  17.8 2.1 copy-start.2
  20.4 1.2 copy-start.3
  24.5 6.2 %copy-start.7 = (bf16[4,2,16,896]{3,2,1,0:T(8,128)(2,1)S(1)}, bf16[4,2,16,896]{3,2,1,0:T(8,128)(2,1)}, u32[]{:S(2)}) copy-start(bf16[4,2,16,896]{3,2,1,0:T(8,128)(2,1)} %param.25) | copy-start | bytes 688132
  24.5 68.1 %all-to-all-start = ((bf16[8,64,1792]{2,1,0:T(8,128)(2,1)}), bf16[8,64,1792]{2,1,0:T(8,128)(2,1)}, u32[]{:S(2)}, u32[]{:S(2)}) async-start(bf16[8,64,1792]{2,1,0:T(8,128)(2,1)} %copy.69), calls=%async_computation | async-start | bytes 3670016 | tf_op jit(solution)/shard_map/all_to_all | solution.py:117
  92.6 2.4 copy-start.6
  97.3 75.2 %all-to-all-start.2 = ((bf16[8,64,1792]{2,1,0:T(8,128)(2,1)}), bf16[8,64,1792]{2,1,0:T(8,128)(2,1)}, u32[]{:S(2)}, u32[]{:S(2)}) async-start(bf16[8,64,1792]{2,1,0:T(8,128)(2,1)} %pad_maximum_fusion), calls=%async_computation.2 | async-start | bytes 3670016 | tf_op jit(solution)/shard_map/all_to_all | solution.py:127
  101.8 8.7 %copy-start.10 = (s32[1,512]{1,0:T(1,128)S(1)}, s32[1,512]{1,0:T(1,128)}, u32[]{:S(2)}) copy-start(s32[1,512]{1,0:T(1,128)} %param.26) | copy-start | bytes 6148
  101.8 8.7 %copy-start.12 = (s32[8]{0:T(128)S(1)}, s32[8]{0:T(128)}, u32[]{:S(2)}) copy-start(s32[8]{0:T(128)} %param.21) | copy-start | bytes 100
  175.3 2.6 copy-start.11
  176.8 1.9 copy-start.4
  184.8 2.1 copy-start.5
  217.6 82.4 %copy-start.9 = (f32[1792]{0:T(1024)S(1)}, f32[1792]{0:T(1024)}, u32[]{:S(2)}) copy-start(f32[1792]{0:T(1024)} %param.27) | copy-start | bytes 21508
  313.8 13.0 %copy-start.1 = (bf16[896,1792]{1,0:T(8,128)(2,1)S(1)}, bf16[896,1792]{1,0:T(8,128)(2,1)}, u32[]{:S(2)}) copy-start(bf16[896,1792]{1,0:T(8,128)(2,1)} %param.20) | copy-start | bytes 9633796
Sparse Core Ops, SparseCore 0:
  10.9 158.5 all-gather.2
  172.4 128.3 all-gather.4
where the time goes:
time: 334 us
  waiting for transfers between devices  121 us (36%)
  blocking collectives  81.8 us (24%)
  matrix products  60.7 us (18%)
  local copies, waits for them, and re-layouts  28.6 us (9%)
  starting transfers between devices  18 us (5%)
  between operations  14.2 us (4%)
  other arithmetic  8.71 us (3%)
    all_to_all x1, blocking collectives, local(): lax.all_to_all(shuffled, ('dp', 'mp'), split_axis=0, concat_axis=0, tiled...  81.8 us
    all_to_all x1, waiting for transfers between devices, local(): lax.all_to_all(deltas, 'mp', split_axis=0, concat_axis=0, tiled=True)  61.7 us
    all_to_all x1, waiting for transfers between devices, local(): lax.all_to_all(outgoing, 'mp', split_axis=0, concat_axis=0, tiled=True)  58.4 us
    dot_general x1, matrix products, local(): upper = jnp.dot(mlp_input, full_up, preferred_element_type=jnp.float32)  13 us
    dot_general x1, matrix products, local(): gate = jnp.dot(mlp_input, full_gate, preferred_element_type=jnp.float32)  12.1 us
    all_to_all x1, starting transfers between devices, local(): lax.all_to_all(chosen, 'mp', split_axis=0, concat_axis=0, tiled=True)  7.28 us
  transfers between devices with their start and end apart: 5, of which 2 were waited for; matrix products, arithmetic and copies ran while one was open for 25% of the time, Pallas kernels for 0%

commit v1 on v0

v1 whole, which is shorter than its diff:
```python
import jax
import jax.numpy as jnp
from jax import lax
from jax.experimental import pallas as pl
from jax.experimental.pallas import tpu as pltpu
from jax.sharding import PartitionSpec as P

EMBED_SPAN = 1792
HEADS = 8
HD = 112
LATENT_BREADTH = 16
REQ_DEV = 8
SLOTR = 64
WINDOW = 32
SINKS = 4


PLUGIN_STRENGTH = 2.0
EPSILON = 1e-05


def normalize(rows_in, gain_vec):
    floated = rows_in.astype(jnp.float32)
    scale = lax.rsqrt(jnp.mean(floated * floated, axis=-1, keepdims=True) + EPSILON)
    return (floated * scale * gain_vec).astype(jnp.bfloat16)


def attend(query, key, value, request_len):
    queries = query.reshape(REQ_DEV, SLOTR, HEADS, HD)
    head_keys = key.reshape(REQ_DEV, SLOTR, HEADS, HD)
    head_values = value.reshape(REQ_DEV, SLOTR, HEADS, HD)
    scores = jnp.einsum(
        "rqhd,rkhd->rhqk", queries, head_keys, preferred_element_type=jnp.float32
    ) * HD ** (-0.5)
    places = jnp.arange(SLOTR)
    query_place = places[:, None]
    key_place = places[None, :]
    allowed = (key_place <= query_place) & (
        (query_place - key_place < WINDOW) | (key_place < SINKS)
    )
    key_live = places[None, :] < request_len[:, None]
    visible_lookup_flags = allowed[None, None, :, :] & key_live[:, None, None, :]
    scores = jnp.where(visible_lookup_flags, scores, -1e30)
    row_max = jnp.max(scores, axis=-1, keepdims=True)
    expo = jnp.where(visible_lookup_flags, jnp.exp(scores - row_max), 0.0)
    softmax_w = (expo / jnp.sum(expo, axis=-1, keepdims=True)).astype(jnp.bfloat16)
    attended = jnp.einsum(
        "rhqk,rkhd->rqhd", softmax_w, head_values, preferred_element_type=jnp.float32
    ).astype(jnp.bfloat16)
    query_live = (places[None, :] < request_len[:, None])[:, :, None, None]
    attended = jnp.where(query_live, attended, jnp.zeros_like(attended))
    return attended.reshape(REQ_DEV * SLOTR, HEADS * HD)


CORES = 2


def gated_kernel(own_ref, sib_ref, go_ref, gs_ref, uo_ref, us_ref, o_ref):
    own = own_ref[...]
    sib = sib_ref[...]
    gate = jnp.dot(own, go_ref[...], preferred_element_type=jnp.float32)
    gate += jnp.dot(sib, gs_ref[...], preferred_element_type=jnp.float32)
    up = jnp.dot(own, uo_ref[...], preferred_element_type=jnp.float32)
    up += jnp.dot(sib, us_ref[...], preferred_element_type=jnp.float32)
    o_ref[...] = (gate * jax.nn.sigmoid(gate) * up).astype(o_ref.dtype)


def gated(own, sib, gate_own, gate_sib, up_own, up_sib):
    rows, depth = own.shape
    width = gate_own.shape[1]
    tile = 512
    act = pl.BlockSpec((rows, depth), lambda i: (0, 0))
    wgt = pl.BlockSpec((depth, tile), lambda i: (0, i))
    return pl.pallas_call(
        gated_kernel,
        out_shape=jax.ShapeDtypeStruct((rows, width), jnp.bfloat16),
        grid=(width // tile,),
        in_specs=[act, act, wgt, wgt, wgt, wgt],
        out_specs=pl.BlockSpec((rows, tile), lambda i: (0, i)),
        compiler_params=pltpu.CompilerParams(vmem_limit_bytes=40 << 20),
        name="gated_units",
    )(own, sib, gate_own, gate_sib, up_own, up_sib)


def local(
    tokens,
    first_norm_gain,
    query_weight,
    key_weight,
    value_weight,
    output_weight,
    lengths,
    request_adapter,
    slot_adapter_ids,
    plugin_shrink_maps,
    plugin_grow_maps,
    device_token_order,
    second_norm_gain,
    gate_weight,
    up_weight,
):
    owner_count = lax.axis_size("mp")
    resident_slots = plugin_shrink_maps.shape[0]
    tok_dev = tokens.shape[0]
    hw_size = query_weight.shape[1]
    every = ("x", "core", "mp")
    swap = [(0, 1), (1, 0)]
    core = lax.axis_index("core")

    gate_own = lax.all_gather(gate_weight, ("x", "mp"), axis=0, tiled=True)
    up_own = lax.all_gather(up_weight, ("x", "mp"), axis=0, tiled=True)
    gate_sib = lax.ppermute(gate_own, "core", swap)
    up_sib = lax.ppermute(up_own, "core", swap)

    matches = (slot_adapter_ids[None, :] == request_adapter[:, None]).astype(jnp.int32)
    slot_ids = jnp.sum(
        matches * jnp.arange(slot_adapter_ids.shape[0], dtype=jnp.int32)[None, :], axis=1
    )
    owner_index = slot_ids // resident_slots
    within = slot_ids % resident_slots
    routing = (jnp.arange(owner_count)[:, None] == owner_index[None, :]).astype(jnp.bfloat16)
    slot_pick = (jnp.arange(resident_slots)[None, :] == within[:, None]).astype(jnp.bfloat16)
    chosen = jnp.dot(routing, slot_pick, preferred_element_type=jnp.float32).astype(jnp.bfloat16)
    chosen_adapter = lax.all_to_all(chosen, "mp", split_axis=0, concat_axis=0, tiled=True)
    maps = jnp.concatenate(
        [
            plugin_shrink_maps.transpose(0, 2, 1),
            plugin_grow_maps.reshape(resident_slots, 2 * LATENT_BREADTH, hw_size),
        ],
        axis=-1,
    )
    outgoing = jnp.einsum(
        "ge,ezc->gzc", chosen_adapter, maps, preferred_element_type=jnp.float32
    ).astype(jnp.bfloat16)
    incoming = lax.all_to_all(outgoing, "mp", split_axis=0, concat_axis=0, tiled=True)
    own_maps = jnp.einsum(
        "or,ozc->rzc", routing, incoming, preferred_element_type=jnp.float32
    ).astype(jnp.bfloat16)

    normed = normalize(tokens, first_norm_gain)
    request_rows = normed.reshape(REQ_DEV, SLOTR, EMBED_SPAN)
    codes = jnp.einsum(
        "rsd,rkd->rsk",
        request_rows,
        own_maps[..., :EMBED_SPAN],
        preferred_element_type=jnp.float32,
    ).astype(jnp.bfloat16)
    delta_q = (
        jnp.einsum(
            "rsk,rkh->rsh",
            codes[..., :LATENT_BREADTH],
            own_maps[:, :LATENT_BREADTH, EMBED_SPAN:],
            preferred_element_type=jnp.float32,
        )
        * PLUGIN_STRENGTH
    ).astype(jnp.bfloat16)
    delta_v = (
        jnp.einsum(
            "rsk,rkh->rsh",
            codes[..., LATENT_BREADTH:],
            own_maps[:, LATENT_BREADTH:, EMBED_SPAN:],
            preferred_element_type=jnp.float32,
        )
        * PLUGIN_STRENGTH
    ).astype(jnp.bfloat16)
    query = (
        jnp.dot(normed, query_weight, preferred_element_type=jnp.float32)
        + delta_q.reshape(tok_dev, hw_size).astype(jnp.float32)
    ).astype(jnp.bfloat16)
    key = jnp.dot(normed, key_weight, preferred_element_type=jnp.float32).astype(jnp.bfloat16)
    value = (
        jnp.dot(normed, value_weight, preferred_element_type=jnp.float32)
        + delta_v.reshape(tok_dev, hw_size).astype(jnp.float32)
    ).astype(jnp.bfloat16)
    attended = attend(query, key, value, lengths)
    residual = (
        tokens.astype(jnp.float32)
        + jnp.dot(attended, output_weight, preferred_element_type=jnp.float32)
    ).astype(jnp.bfloat16)
    order = (device_token_order[0][:, None] == jnp.arange(tok_dev)[None, :]).astype(jnp.bfloat16)
    shuffled = jnp.dot(order, residual, preferred_element_type=jnp.float32).astype(jnp.bfloat16)
    regrouped = lax.all_to_all(shuffled, every, split_axis=0, concat_axis=0, tiled=True)
    mlp_input = normalize(regrouped, second_norm_gain)
    by_core = mlp_input.reshape(tok_dev, lax.axis_size("x"), CORES, -1)
    even = by_core[:, :, 0].reshape(tok_dev, -1)
    odd = by_core[:, :, 1].reshape(tok_dev, -1)
    own = jnp.where(core == 0, even, odd)
    sib = jnp.where(core == 0, odd, even)
    hidden = gated(own, sib, gate_own, gate_sib, up_own, up_sib)
    return (residual, hidden)


def solution(mesh):
    dp, mp = mesh.devices.shape
    fine = jax.sharding.Mesh(mesh.devices.reshape(dp // CORES, CORES, mp), ("x", "core", "mp"))
    rows = ("x", "core", "mp")
    return jax.shard_map(
        local,
        mesh=fine,
        in_specs=(
            P(rows, None),
            P(),
            P(),
            P(),
            P(),
            P(),
            P(rows),
            P(rows),
            P(),
            P("mp", None, None),
            P("mp", None, None, None),
            P(rows, None),
            P(),
            P(rows, None),
            P(rows, None),
        ),
        out_specs=(P(rows, None), P(rows, None)),
        check_vma=False,
    )
```

time: 334 us -> 334 us (level)
  blocking collectives: 81.8 us -> 0 us
  waiting for transfers between devices: 121 us -> 195 us
  matrix products: 60.7 us -> 32.7 us
  Pallas kernels: 0 us -> 19.6 us
  local copies, waits for them, and re-layouts: 28.6 us -> 42 us
  other arithmetic: 8.71 us -> 15.1 us
    all_gather x2, waiting for transfers between devices: 0.01 us -> 107 us  [the longest x1 96.6 us: local(): gate_own = lax.all_gather(gate_weight, ('x', 'mp'), axis=0, tiled=True)]
    all_to_all x1 -> x0, blocking collectives: 81.8 us -> none  [local(): lax.all_to_all(shuffled, ('dp', 'mp'), split_axis=0, concat_axis=0, tiled...]
    dot_general x9 -> x6, matrix products: 35.2 us -> 9.11 us  [the longest x1 3.9 us: local(): jnp.dot(order, residual, preferred_element_type=jnp.float32)]
    all_to_all x1, waiting for transfers between devices: 58.4 us -> 38.5 us  [local(): lax.all_to_all(outgoing, 'mp', split_axis=0, concat_axis=0, tiled=True)]
    pallas_call x0 -> x1, Pallas kernels: none -> 19.6 us  [gated(): pl.pallas_call(gated_kernel, out_shape=jax.ShapeDtypeStruct((rows, width)...]
    all_to_all x1, waiting for transfers between devices: 61.7 us -> 44.4 us  [local(): lax.all_to_all(shuffled, every, split_axis=0, concat_axis=0, tiled=True)]
    select_n x0 -> x4, local copies, waits for them, and re-layouts: none -> 9.13 us  [the longest x2 6.13 us: local(): sib = jnp.where(core == 0, odd, even)]
    unnamed x26 -> x34, local copies, waits for them, and re-layouts: 2.84 us -> 11.3 us
  transfers between devices with their start and end apart: 5 -> 7, of which waited for: 2 -> 5; matrix products, arithmetic and copies ran while one was open for 25% -> 25% of each run, Pallas kernels for 0% -> 0%
where the time goes in v1:
time: 334 us; the launch traced here: 333 us
  waiting for transfers between devices  195 us (58%)
  local copies, waits for them, and re-layouts  42 us (13%)
  matrix products  32.7 us (10%)
  Pallas kernels  19.6 us (6%)
  other arithmetic  15.1 us (5%)
  starting transfers between devices  14.8 us (4%)
  between operations  14.3 us (4%)
    all_gather x1, waiting for transfers between devices, local(): gate_own = lax.all_gather(gate_weight, ('x', 'mp'), axis=0, tiled=True)  96.6 us
    all_to_all x1, waiting for transfers between devices, local(): lax.all_to_all(shuffled, every, split_axis=0, concat_axis=0, tiled=True)  44.4 us
    all_to_all x1, waiting for transfers between devices, local(): lax.all_to_all(outgoing, 'mp', split_axis=0, concat_axis=0, tiled=True)  38.5 us
    pallas_call x1, Pallas kernels, gated(): pl.pallas_call(gated_kernel, out_shape=jax.ShapeDtypeStruct((rows, width)...  19.6 us
    unnamed x34, local copies, waits for them, and re-layouts  11.3 us
    all_gather x1, waiting for transfers between devices, local(): up_own = lax.all_gather(up_weight, ('x', 'mp'), axis=0, tiled=True)  10.5 us
    all_to_all x1, starting transfers between devices, local(): lax.all_to_all(chosen, 'mp', split_axis=0, concat_axis=0, tiled=True)  7.28 us
  transfers between devices with their start and end apart: 7, of which 5 were waited for; matrix products, arithmetic and copies ran while one was open for 25% of the time, Pallas kernels for 0%

profile of v1, /device:TPU:0, one launch (start us, length us, event | category | flops | bytes accessed | tf_op | source)
XLA Modules:
  0.0 333.0 jit_solution(13140188764013692128)
XLA Ops:
  7.2 0.0 copy-start
  7.2 0.0 all-gather.5.cloned.1.call-start
  7.2 0.7 all-gather.5.cloned.1.call-update
  7.9 0.0 all-gather.3.cloned.1.call-start
  8.0 0.7 all-gather.3.cloned.1.call-update
  8.7 0.9 select_reduce_fusion
  9.5 0.3 fusion.11
  9.8 0.7 copy.54
  10.5 7.3 %all-to-all-start = ((bf16[8,1,4]{2,1,0:T(2,128)(2,1)}), bf16[8,1,4]{2,1,0:T(2,128)(2,1)S(1)}, u32[]{:S(2)}, u32[]{:S(2)}) async-start(bf16[8,1,4]{2,1,0:T(2,128)(2,1)} %copy.54), calls=%async_computation | async-start | bytes 8192 | tf_op jit(solution)/shard_map/all_to_all | solution.py:124
  17.8 1.1 copy.57
  18.8 2.1 copy.96
  21.0 3.2 all-to-all-done
  24.2 0.1 copy.55
  24.2 1.6 convolution_convert_fusion.1
  25.9 1.2 copy.58
  27.1 4.4 %all-to-all-start.1 = ((bf16[8,32,2688]{2,1,0:T(8,128)(2,1)}), bf16[8,32,2688]{2,1,0:T(8,128)(2,1)}, u32[]{:S(2)}, u32[]{:S(2)}) async-start(bf16[8,32,2688]{2,1,0:T(8,128)(2,1)} %copy.58), calls=%async_computation.1 | async-start | bytes 2752512 | tf_op jit(solution)/shard_map/all_to_all | solution.py:135
  31.5 0.0 copy-start.6
  31.5 2.1 fusion.1
  33.6 0.5 fusion.3
  34.1 0.0 copy-start.7
  34.1 1.2 copy-done.7
  35.4 0.8 copy-done.12
  36.2 3.0 convolution_convert_fusion.4
  39.2 3.1 reshape.204
  42.3 0.1 iota_compare_fusion.6
  42.4 0.1 fusion.29
  42.5 0.8 broadcast_and_fusion
  43.3 38.5 %all-to-all-done.1 = bf16[8,32,2688]{2,1,0:T(8,128)(2,1)} async-done(((bf16[8,32,2688]{2,1,0:T(8,128)(2,1)}), bf16[8,32,2688]{2,1,0:T(8,128)(2,1)}, u32[]{:S(2)}, u32[]{:S(2)}) %all-to-all-start.1) | async-done | bytes 1376288 | tf_op jit(solution)/shard_map/all_to_all | solution.py:135
  81.8 2.1 convolution_convert_fusion
  83.9 0.1 slice.28
  84.0 0.0 copy-start.13
  84.1 0.6 convolution_convert_fusion.5
  84.7 0.4 multiply_convert_fusion.1
  85.1 0.8 copy-done.13
  86.0 3.0 fusion.6
  88.9 3.1 reshape.203
  92.1 0.4 multiply_convert_fusion.2
  92.5 5.5 %fusion.7 = bf16[512,896]{1,0:T(8,128)(2,1)} fusion(bf16[512,896]{1,0:T(8,128)(2,1)S(1)} %bitcast.40, bf16[512,1792]{1,0:T(8,128)(2,1)} %copy-done.7, bf16[1792,896]{1,0:T(8,128)(2,1)} %param.19), kind=kOutput, calls=%fused_computation.22 | convolution fusion | flops 1645543424 | bytes 6881280 | tf_op jit(solution)/shard_map/dot_general | solution.py:172
  98.0 3.1 reshape.202
  101.2 4.2 %fusion.41 = (f32[8,8,64]{2,1,0:T(8,128)S(1)}, f32[8,8,64,64]{2,3,1,0:T(8,128)}) fusion(pred[8,64,64]{1,2,0:T(8,128)(4,1)S(1)} %copy-done.9, bf16[8,64,8,112]{3,2,1,0:T(8,128)(2,1)} %reshape.204, bf16[8,64,8,112]{3,2,1,0:T(8,128)(2,1)} %reshape.203), kind=kOutput, calls=%fused_computation.78 | convolution fusion | flops 60031040 | bytes 2932736 | tf_op jit(solution)/shard_map/sub | solution.py:45
  105.3 2.5 fusion.10
  107.8 1.7 copy.67
  109.5 2.7 reshape.205
  112.2 5.1 %fusion.4 = bf16[512,1792]{1,0:T(8,128)(2,1)} fusion(bf16[512,1792]{1,0:T(8,128)(2,1)} %param.15, bf16[512,896]{1,0:T(8,128)(2,1)} %reshape.205, bf16[896,1792]{1,0:T(8,128)(2,1)S(1)} %copy-done), kind=kOutput, calls=%fused_computation.12 | convolution fusion | flops 1646919680 | bytes 7798784 | tf_op jit(solution)/shard_map/dot_general | solution.py:178
  117.4 10.5 %all-gather.5.cloned.1.call-done.uo_ref = bf16[896,3584]{1,0:T(8,128)(2,1)} async-done(((bf16[56,3584]{1,0:T(8,128)(2,1)}), bf16[896,3584]{1,0:T(8,128)(2,1)}) %all-gather.5.cloned.1.call-update) | async-done | bytes 6422544 | tf_op jit(solution)/shard_map/all_gather | solution.py:111
  127.8 0.0 collective-permute-start.1
  127.9 96.6 %all-gather.3.cloned.1.call-done.go_ref = bf16[896,3584]{1,0:T(8,128)(2,1)} async-done(((bf16[56,3584]{1,0:T(8,128)(2,1)}), bf16[896,3584]{1,0:T(8,128)(2,1)}) %all-gather.3.cloned.1.call-update) | async-done | bytes 6422544 | tf_op jit(solution)/shard_map/all_gather | solution.py:110
  224.5 3.9 %convolution_convert_fusion.2 = bf16[512,1792]{1,0:T(8,128)(2,1)} fusion(bf16[512,1792]{1,0:T(8,128)(2,1)} %fusion.4, s32[512]{0:T(512)S(1)} %bitcast.44), kind=kOutput, calls=%fused_computation.14 | convolution fusion | flops 940703744 | bytes 3672064 | tf_op jit(solution)/shard_map/dot_general | solution.py:181
  228.4 3.0 all-to-all-start.2
  231.4 0.1 mul.77
  231.5 44.4 %all-to-all-done.2 = bf16[32,16,1792]{2,1,0:T(8,128)(2,1)S(1)} async-done(((bf16[32,16,1792]{2,1,0:T(8,128)(2,1)}), bf16[32,16,1792]{2,1,0:T(8,128)(2,1)S(1)}, u32[]{:S(2)}, u32[]{:S(2)}) %all-to-all-start.2) | async-done | bytes 1835040 | tf_op jit(solution)/shard_map/all_to_all | solution.py:182
  275.9 0.4 multiply_reduce_fusion
  276.3 0.1 rsqrt.21
  276.4 5.5 %reshape.208 = f32[512,2,2,448]{3,2,1,0:T(2,128)} reshape(bf16[32,16,1792]{2,1,0:T(8,128)(2,1)S(1)} %all-to-all-done.2) | data formatting | bytes 5505024 | tf_op jit(solution)/shard_map/convert_element_type | solution.py:23
  281.9 4.4 %multiply_convert_fusion = bf16[512,2,2,448]{3,2,1,0:T(2,128)(2,1)S(1)} fusion(f32[512,2,2,448]{3,2,1,0:T(2,128)} %reshape.208, f32[512]{0:T(512)S(1)} %rsqrt.21, f32[2,2,448]{2,1,0:T(2,128)S(1)} %mul.77), kind=kLoop, calls=%fused_computation.4 | loop fusion | flops 2752512 | bytes 5514240 | tf_op jit(solution)/shard_map/convert_element_type | solution.py:25
  286.3 5.9 %broadcast_select_fusion = (bf16[512,2,1,448]{3,2,1,0:T(2,128)(2,1)}, bf16[512,2,1,448]{3,2,1,0:T(2,128)(2,1)}) fusion(pred[]{:T(512)S(6)} %eq.69, bf16[512,2,2,448]{3,2,1,0:T(2,128)(2,1)S(1)} %multiply_convert_fusion), kind=kLoop, calls=%fused_computation.5 | loop fusion | flops 917504 | bytes 3670017 | tf_op jit(solution)/shard_map/jit(_where)/select_n | solution.py:188
  292.3 4.8 %copy.69 = bf16[512,2,1,448]{0,3,1,2:T(8,128)(2,1)S(1)} copy(bf16[512,2,1,448]{3,2,1,0:T(2,128)(2,1)} %get-tuple-element.2) | data formatting | bytes 1835008 | tf_op jit(solution)/shard_map/jit(_where)/select_n | solution.py:188
  297.1 1.3 copy.71.sib_ref
  298.4 1.7 copy.68
  300.1 1.3 copy.70.own_ref
  301.4 2.8 copy-done.2
  304.2 1.2 copy-done.3
  305.4 1.2 copy-done.4
  306.6 19.6 %gated_units.1 = bf16[512,3584]{1,0:T(8,128)(2,1)} custom-call(bf16[512,896]{1,0:T(8,128)(2,1)S(1)} %copy-done.4, bf16[512,896]{1,0:T(8,128)(2,1)S(1)} %copy-done.3, bf16[896,3584]{1,0:T(8,128)(2,1)S(1)} %copy-done.2, bf16[896,3584]{1,0:T(8,128)(2,1)} %collective-permute-done.gs_ref, bf16[896,3584]{1,0:T(8,128)(2,1)} %all-gather.5.cloned.1.call-done.uo_ref, ...), custom_call_target="tpu_custom_call" | custom-call | tf_op jit(solution)/shard_map/gated_units/pallas_call | solution.py:74
  (30 shorter events, 0.1 us)
Async XLA Ops:
  7.2 105.1 %copy-start = (bf16[896,1792]{1,0:T(8,128)(2,1)S(1)}, bf16[896,1792]{1,0:T(8,128)(2,1)}, u32[]{:S(2)}) copy-start(bf16[896,1792]{1,0:T(8,128)(2,1)} %param.20) | copy-start | bytes 9633796
  7.2 120.7 %all-gather.5.cloned.1.call-start = ((), (), s32[]{:S(2)}) async-start(), calls=%async_computation.4 | async-start | bytes 6823936 | tf_op jit(solution)/shard_map/all_gather | solution.py:111
  7.9 216.6 %all-gather.3.cloned.1.call-start = ((), (), s32[]{:S(2)}) async-start(), calls=%async_computation.3 | async-start | bytes 6823936 | tf_op jit(solution)/shard_map/all_gather | solution.py:110
  10.5 13.7 %all-to-all-start = ((bf16[8,1,4]{2,1,0:T(2,128)(2,1)}), bf16[8,1,4]{2,1,0:T(2,128)(2,1)S(1)}, u32[]{:S(2)}, u32[]{:S(2)}) async-start(bf16[8,1,4]{2,1,0:T(2,128)(2,1)} %copy.54), calls=%async_computation | async-start | bytes 8192 | tf_op jit(solution)/shard_map/all_to_all | solution.py:124
  27.1 6.5 %copy-start.10 = (f32[1792]{0:T(1024)S(1)}, f32[1792]{0:T(1024)}, u32[]{:S(2)}) copy-start(f32[1792]{0:T(1024)} %param.16) | copy-start | bytes 21508
  27.1 54.7 %all-to-all-start.1 = ((bf16[8,32,2688]{2,1,0:T(8,128)(2,1)}), bf16[8,32,2688]{2,1,0:T(8,128)(2,1)}, u32[]{:S(2)}, u32[]{:S(2)}) async-start(bf16[8,32,2688]{2,1,0:T(8,128)(2,1)} %copy.58), calls=%async_computation.1 | async-start | bytes 2752512 | tf_op jit(solution)/shard_map/all_to_all | solution.py:135
  31.5 2.1 copy-start.6
  33.6 2.6 copy-start.12
  34.1 1.2 copy-start.7
  36.2 6.2 %copy-start.15 = (s32[8]{0:T(128)S(1)}, s32[8]{0:T(128)}, u32[]{:S(2)}) copy-start(s32[8]{0:T(128)} %param.21) | copy-start | bytes 100
  81.8 2.2 copy-start.8
  84.0 1.9 copy-start.13
  92.5 8.7 %copy-start.9 = (pred[8,64,64]{1,2,0:T(8,128)(4,1)S(1)}, pred[8,64,64]{1,2,0:T(8,128)(4,1)}, u32[]{:S(2)}) copy-start(pred[8,64,64]{1,2,0:T(8,128)(4,1)} %broadcast_and_fusion) | copy-start | bytes 98308
  112.2 112.3 %copy-start.14 = (s32[1,512]{1,0:T(1,128)S(1)}, s32[1,512]{1,0:T(1,128)}, u32[]{:S(2)}) copy-start(s32[1,512]{1,0:T(1,128)} %param.26) | copy-start | bytes 6148
  127.8 173.6 %collective-permute-start.1 = (bf16[896,3584]{1,0:T(8,128)(2,1)}, bf16[896,3584]{1,0:T(8,128)(2,1)}, u32[]{:S(2)}, u32[]{:S(2)}) collective-permute-start(bf16[896,3584]{1,0:T(8,128)(2,1)} %all-gather.5.cloned.1.call-done.uo_ref), channel_id=1, source_target_pairs={{0,8},{8,0},{1,9},{9,1},{2,10},{10,2},{3,11},{11,3},{4,12},{12,4},... | collective-permute-start | bytes 19267592 | tf_op jit(solution)/shard_map/ppermute | solution.py:113
  224.5 76.9 %collective-permute-start = (bf16[896,3584]{1,0:T(8,128)(2,1)}, bf16[896,3584]{1,0:T(8,128)(2,1)}, u32[]{:S(2)}, u32[]{:S(2)}) collective-permute-start(bf16[896,3584]{1,0:T(8,128)(2,1)} %all-gather.3.cloned.1.call-done.go_ref), channel_id=1, source_target_pairs={{0,8},{8,0},{1,9},{9,1},{2,10},{10,2},{3,11},{11,3},{4,12},{12,4},... | collective-permute-start | bytes 19267592 | tf_op jit(solution)/shard_map/ppermute | solution.py:112
  228.4 3.0 copy-start.11
  228.4 47.5 %all-to-all-start.2 = ((bf16[32,16,1792]{2,1,0:T(8,128)(2,1)}), bf16[32,16,1792]{2,1,0:T(8,128)(2,1)S(1)}, u32[]{:S(2)}, u32[]{:S(2)}) async-start(bf16[32,16,1792]{2,1,0:T(8,128)(2,1)} %bitcast.39), calls=%async_computation.2 | async-start | bytes 3670016 | tf_op jit(solution)/shard_map/all_to_all | solution.py:182
  292.3 6.1 %copy-start.5 = (bf16[512,2,1,448]{3,2,1,0:T(2,128)(2,1)S(1)}, bf16[512,2,1,448]{3,2,1,0:T(2,128)(2,1)}, u32[]{:S(2)}) copy-start(bf16[512,2,1,448]{3,2,1,0:T(2,128)(2,1)} %get-tuple-element.3) | copy-start | bytes 2752516
  301.4 2.8 copy-start.2
  304.2 1.2 copy-start.3
  305.4 1.2 copy-start.4
  306.6 19.6 %copy-start.1 = (bf16[896,1792]{1,0:T(8,128)(2,1)S(1)}, bf16[896,1792]{1,0:T(8,128)(2,1)}, u32[]{:S(2)}) copy-start(bf16[896,1792]{1,0:T(8,128)(2,1)} %param.20) | copy-start | bytes 9633796
Sparse Core Ops, SparseCore 0:
  10.7 117.0 all-gather.4
  130.6 93.8 all-gather.2

commit v2 on v1

--- a/solution.py
+++ b/solution.py
@@ -1,3 +1,5 @@
+import functools
+
 import jax
 import jax.numpy as jnp
 from jax import lax
@@ -55,31 +57,62 @@
 CORES = 2
 
 
-def gated_kernel(own_ref, sib_ref, go_ref, gs_ref, uo_ref, us_ref, o_ref):
-    own = own_ref[...]
-    sib = sib_ref[...]
-    gate = jnp.dot(own, go_ref[...], preferred_element_type=jnp.float32)
-    gate += jnp.dot(sib, gs_ref[...], preferred_element_type=jnp.float32)
-    up = jnp.dot(own, uo_ref[...], preferred_element_type=jnp.float32)
-    up += jnp.dot(sib, us_ref[...], preferred_element_type=jnp.float32)
+def gated_kernel(blocks, spots_ref, rows_ref, gain_ref, *refs):
+    gate_refs = refs[: 2 * blocks]
+    up_refs = refs[2 * blocks : 2 * blocks + 2]
+    o_ref, act = refs[2 * blocks + 2 :]
+    depth = act.shape[2]
+
+    @pl.when(pl.program_id(0) == 0)
+    def _():
+        @pl.loop(0, rows_ref.shape[0], step=64)
+        def _(r):
+            part = pl.ds(pl.multiple_of(r, 64), 64)
+            wide = rows_ref[part, :].astype(jnp.float32)
+            scale = lax.rsqrt(jnp.mean(wide * wide, axis=-1, keepdims=True) + EPSILON)
+            done = (wide * scale * gain_ref[...]).astype(jnp.bfloat16)
+            for k in range(2 * blocks):
+                act[k, part, :] = done[:, k * depth : (k + 1) * depth]
+
+    gate = None
+    up = None
+    for k in range(2 * blocks):
+        side, at = divmod(k, blocks)
+        term = jnp.dot(
+            act[spots_ref[k]], gate_refs[k][...], preferred_element_type=jnp.float32
+        )
+        gate = term if gate is None else gate + term
+        term = jnp.dot(
+            act[spots_ref[2 * blocks + k]],
+            up_refs[side][at * depth : (at + 1) * depth, :],
+            preferred_element_type=jnp.float32,
+        )
+        up = term if up is None else up + term
     o_ref[...] = (gate * jax.nn.sigmoid(gate) * up).astype(o_ref.dtype)
 
 
-def gated(own, sib, gate_own, gate_sib, up_own, up_sib):
-    rows, depth = own.shape
-    width = gate_own.shape[1]
+def gated(regrouped, gain, spots, gates, ups):
+    rows, width_in = regrouped.shape
+    width = gates[0].shape[1]
+    blocks = len(gates) // 2
+    depth = gates[0].shape[0]
     tile = 512
-    act = pl.BlockSpec((rows, depth), lambda i: (0, 0))
-    wgt = pl.BlockSpec((depth, tile), lambda i: (0, i))
+    whole = lambda i, spots: (0, 0)
+    strip = lambda i, spots: (0, i)
     return pl.pallas_call(
-        gated_kernel,
+        functools.partial(gated_kernel, blocks),
         out_shape=jax.ShapeDtypeStruct((rows, width), jnp.bfloat16),
-        grid=(width // tile,),
-        in_specs=[act, act, wgt, wgt, wgt, wgt],
-        out_specs=pl.BlockSpec((rows, tile), lambda i: (0, i)),
+        grid_spec=pltpu.PrefetchScalarGridSpec(
+            num_scalar_prefetch=1,
+            grid=(width // tile,),
+            in_specs=[pl.BlockSpec((rows, width_in), whole), pl.BlockSpec((1, width_in), whole)]
+            + [pl.BlockSpec((w.shape[0], tile), strip) for w in (*gates, *ups)],
+            out_specs=pl.BlockSpec((rows, tile), strip),
+            scratch_shapes=[pltpu.VMEM((2 * blocks, rows, depth), jnp.bfloat16)],
+        ),
         compiler_params=pltpu.CompilerParams(vmem_limit_bytes=40 << 20),
         name="gated_units",
-    )(own, sib, gate_own, gate_sib, up_own, up_sib)
+    )(spots, regrouped, gain[None, :], *gates, *ups)
 
 
 def local(
@@ -107,10 +140,11 @@
     swap = [(0, 1), (1, 0)]
     core = lax.axis_index("core")
 
-    gate_own = lax.all_gather(gate_weight, ("x", "mp"), axis=0, tiled=True)
+    here = lax.axis_index("x")
+    span = lax.axis_size("x")
+    onward = [(i, (i + 1) % span) for i in range(span)]
+    gate_own = lax.all_gather(gate_weight, "mp", axis=0, tiled=True)
     up_own = lax.all_gather(up_weight, ("x", "mp"), axis=0, tiled=True)
-    gate_sib = lax.ppermute(gate_own, "core", swap)
-    up_sib = lax.ppermute(up_own, "core", swap)
 
     matches = (slot_adapter_ids[None, :] == request_adapter[:, None]).astype(jnp.int32)
     slot_ids = jnp.sum(
@@ -172,21 +206,35 @@
         jnp.dot(normed, value_weight, preferred_element_type=jnp.float32)
         + delta_v.reshape(tok_dev, hw_size).astype(jnp.float32)
     ).astype(jnp.bfloat16)
+    gate_own, key = lax.optimization_barrier((gate_own, key))
+    gate_parts = [gate_own]
+    for _ in range(span - 1):
+        gate_parts.append(lax.ppermute(gate_parts[-1], "x", onward))
     attended = attend(query, key, value, lengths)
     residual = (
         tokens.astype(jnp.float32)
         + jnp.dot(attended, output_weight, preferred_element_type=jnp.float32)
     ).astype(jnp.bfloat16)
-    order = (device_token_order[0][:, None] == jnp.arange(tok_dev)[None, :]).astype(jnp.bfloat16)
-    shuffled = jnp.dot(order, residual, preferred_element_type=jnp.float32).astype(jnp.bfloat16)
-    regrouped = lax.all_to_all(shuffled, every, split_axis=0, concat_axis=0, tiled=True)
-    mlp_input = normalize(regrouped, second_norm_gain)
-    by_core = mlp_input.reshape(tok_dev, lax.axis_size("x"), CORES, -1)
-    even = by_core[:, :, 0].reshape(tok_dev, -1)
-    odd = by_core[:, :, 1].reshape(tok_dev, -1)
-    own = jnp.where(core == 0, even, odd)
-    sib = jnp.where(core == 0, odd, even)
-    hidden = gated(own, sib, gate_own, gate_sib, up_own, up_sib)
+    places = device_token_order.reshape(-1, tok_dev // lax.axis_size(every))
+    half = places.shape[1] // 2
+    halves = []
+    for picked in (places[:, :half], places[:, half:]):
+        chosen_rows = picked.reshape(-1, 1) == jnp.arange(tok_dev)[None, :]
+        part = jnp.dot(
+            chosen_rows.astype(jnp.bfloat16), residual, preferred_element_type=jnp.float32
+        ).astype(jnp.bfloat16)
+        part = part.reshape(places.shape[0], half, EMBED_SPAN)
+        halves.append(lax.all_to_all(part, every, split_axis=0, concat_axis=0, tiled=True))
+    gate_parts, up_own, halves[0] = lax.optimization_barrier((gate_parts, up_own, halves[0]))
+    regrouped = jnp.concatenate(halves, axis=1).reshape(tok_dev, EMBED_SPAN)
+    gate_parts = gate_parts + [lax.ppermute(part, "core", swap) for part in gate_parts]
+    up_sib = lax.ppermute(up_own, "core", swap)
+    ahead = jnp.arange(span)
+    walk = (here - ahead + span) % span
+    spots = jnp.concatenate(
+        [walk * CORES + core, walk * CORES + 1 - core, ahead * CORES + core, ahead * CORES + 1 - core]
+    ).astype(jnp.int32)
+    hidden = gated(regrouped, second_norm_gain, spots, gate_parts, [up_own, up_sib])
     return (residual, hidden)
 
 

time: 334 us -> 298 us (0.89)
  waiting for transfers between devices: 195 us -> 79.8 us
  blocking collectives: 0 us -> 99.9 us
  local copies, waits for them, and re-layouts: 42 us -> 25.1 us
  other arithmetic: 15.1 us -> 7.51 us
    all_to_all x0 -> x1, blocking collectives: none -> 99.9 us  [local(): lax.all_to_all(part, every, split_axis=0, concat_axis=0, tiled=True)]
    all_gather x1, waiting for transfers between devices: 96.6 us -> 0.01 us  [local(): gate_own = lax.all_gather(gate_weight, 'mp', axis=0, tiled=True)]
    all_to_all x1, waiting for transfers between devices: 44.4 us -> 24.6 us  [local(): lax.all_to_all(part, every, split_axis=0, concat_axis=0, tiled=True)]
    select_n x4 -> x0, local copies, waits for them, and re-layouts: 9.13 us -> none  [the longest x2 6.13 us: local(): sib = jnp.where(core == 0, odd, even)]
    select_n x1 -> x0, other arithmetic: 5.92 us -> none  [local(): sib = jnp.where(core == 0, odd, even)]
    convert_element_type x1 -> x0, local copies, waits for them, and re-layouts: 5.54 us -> none  [normalize(): floated = rows_in.astype(jnp.float32)]
    all_to_all x1, waiting for transfers between devices: 38.5 us -> 43.7 us  [local(): lax.all_to_all(outgoing, 'mp', split_axis=0, concat_axis=0, tiled=True)]
    convert_element_type x2 -> x1, other arithmetic: 4.9 us -> 0.48 us  [normalize(): return (floated * scale * gain_vec).astype(jnp.bfloat16)]
  transfers between devices with their start and end apart: 7 -> 9, of which waited for: 5 -> 4; matrix products, arithmetic and copies ran while one was open for 25% -> 20% of each run, Pallas kernels for 0% -> 0%
where the time goes in v2:
time: 298 us; the launch traced here: 297 us
  blocking collectives  99.9 us (34%)
  waiting for transfers between devices  79.8 us (27%)
  matrix products  31.1 us (10%)
  local copies, waits for them, and re-layouts  25.1 us (8%)
  Pallas kernels  21.8 us (7%)
  starting transfers between devices  17.6 us (6%)
  between operations  14.3 us (5%)
  other arithmetic  7.51 us (3%)
    all_to_all x1, blocking collectives, local(): lax.all_to_all(part, every, split_axis=0, concat_axis=0, tiled=True)  99.9 us
    all_to_all x1, waiting for transfers between devices, local(): lax.all_to_all(outgoing, 'mp', split_axis=0, concat_axis=0, tiled=True)  43.7 us
    all_to_all x1, waiting for transfers between devices, local(): lax.all_to_all(part, every, split_axis=0, concat_axis=0, tiled=True)  24.6 us
    pallas_call x1, Pallas kernels, gated(): pl.pallas_call(functools.partial(gated_kernel, blocks), out_shape=jax.Sha...  21.8 us
    all_gather x1, waiting for transfers between devices, local(): up_own = lax.all_gather(up_weight, ('x', 'mp'), axis=0, tiled=True)  8.88 us
    unnamed x27, local copies, waits for them, and re-layouts  8.79 us
    all_to_all x1, starting transfers between devices, local(): lax.all_to_all(chosen, 'mp', split_axis=0, concat_axis=0, tiled=True)  7.28 us
  transfers between devices with their start and end apart: 9, of which 4 were waited for; matrix products, arithmetic and copies ran while one was open for 20% of the time, Pallas kernels for 0%

profile of v2, /device:TPU:0, one launch (start us, length us, event | category | flops | bytes accessed | tf_op | source)
XLA Modules:
  0.0 297.1 jit_solution(15350436867182571826)
XLA Ops:
  7.2 0.0 copy-start
  7.2 0.0 all-gather.3.cloned.1.call-start
  7.2 0.7 all-gather.3.cloned.1.call-update
  7.9 0.0 all-gather.5.cloned.1.call-start
  8.0 0.7 all-gather.5.cloned.1.call-update
  8.7 0.9 select_reduce_fusion
  9.5 0.3 fusion.13
  9.8 0.7 copy.46
  10.5 7.3 %all-to-all-start = ((bf16[8,1,4]{2,1,0:T(2,128)(2,1)}), bf16[8,1,4]{2,1,0:T(2,128)(2,1)S(1)}, u32[]{:S(2)}, u32[]{:S(2)}) async-start(bf16[8,1,4]{2,1,0:T(2,128)(2,1)} %copy.46), calls=%async_computation | async-start | bytes 8192 | tf_op jit(solution)/shard_map/all_to_all | solution.py:158
  17.8 0.5 broadcast.198
  18.3 1.3 reduce.3
  19.6 0.1 reshape.183
  19.7 1.1 copy.49
  20.8 2.2 copy.84
  22.9 1.2 all-to-all-done
  24.2 0.1 copy.47
  24.3 1.6 convolution_convert_fusion.1
  25.9 1.2 copy.50
  27.1 4.9 %all-to-all-start.1 = ((bf16[8,32,2688]{2,1,0:T(8,128)(2,1)}), bf16[8,32,2688]{2,1,0:T(8,128)(2,1)}, u32[]{:S(2)}, u32[]{:S(2)}) async-start(bf16[8,32,2688]{2,1,0:T(8,128)(2,1)} %copy.50), calls=%async_computation.1 | async-start | bytes 2752512 | tf_op jit(solution)/shard_map/all_to_all | solution.py:169
  32.0 0.1 fusion.47
  32.1 0.1 eq.82
  32.2 0.0 copy-start.3
  32.2 0.1 iota_compare_fusion.8
  32.3 2.1 fusion.1
  34.3 0.1 fusion.32
  34.4 0.8 broadcast_and_fusion
  35.2 0.5 fusion.3
  35.7 0.0 copy-start.4
  35.7 1.2 copy-done.4
  36.9 0.8 copy-done.9
  37.8 3.1 %convolution_convert_fusion.5 = bf16[512,896]{1,0:T(8,128)(2,1)} fusion(bf16[512,1792]{1,0:T(8,128)(2,1)S(1)} %fusion.3, bf16[1792,896]{1,0:T(8,128)(2,1)S(1)} %copy-done.9), kind=kOutput, calls=%fused_computation.26 | convolution fusion | flops 1644625920 | bytes 5963776 | tf_op jit(solution)/shard_map/dot_general | solution.py:204
  40.8 43.7 %all-to-all-done.1 = bf16[8,32,2688]{2,1,0:T(8,128)(2,1)} async-done(((bf16[8,32,2688]{2,1,0:T(8,128)(2,1)}), bf16[8,32,2688]{2,1,0:T(8,128)(2,1)}, u32[]{:S(2)}, u32[]{:S(2)}) %all-to-all-start.1) | async-done | bytes 1376288 | tf_op jit(solution)/shard_map/all_to_all | solution.py:169
  84.5 2.0 convolution_convert_fusion
  86.5 0.0 copy-start.5
  86.5 0.1 slice.28
  86.6 1.4 copy-done.5
  88.0 0.6 convolution_convert_fusion.6
  88.6 0.4 multiply_convert_fusion
  89.1 0.9 copy-done.10
  89.9 3.0 %fusion.8 = bf16[512,896]{1,0:T(8,128)(2,1)} fusion(bf16[512,896]{1,0:T(8,128)(2,1)S(1)} %bitcast.41, bf16[512,1792]{1,0:T(8,128)(2,1)S(1)} %copy-done.5, bf16[1792,896]{1,0:T(8,128)(2,1)S(1)} %copy-done.10), kind=kOutput, calls=%fused_computation.20 | convolution fusion | flops 1645543424 | bytes 6881280 | tf_op jit(solution)/shard_map/dot_general | solution.py:201
  92.9 3.1 %reshape.180 = bf16[8,64,8,112]{3,2,1,0:T(8,128)(2,1)} reshape(bf16[512,896]{1,0:T(8,128)(2,1)} %fusion.8) | data formatting | bytes 1835008 | tf_op jit(solution)/shard_map/reshape | solution.py:31
  96.1 0.4 multiply_convert_fusion.1
  96.5 5.5 %fusion.9 = bf16[512,896]{1,0:T(8,128)(2,1)} fusion(bf16[512,896]{1,0:T(8,128)(2,1)S(1)} %bitcast.40, bf16[512,1792]{1,0:T(8,128)(2,1)} %copy-done.4, bf16[1792,896]{1,0:T(8,128)(2,1)} %param.19), kind=kOutput, calls=%fused_computation.22 | convolution fusion | flops 1645543424 | bytes 6881280 | tf_op jit(solution)/shard_map/dot_general | solution.py:206
  102.0 3.2 %reshape.179 = bf16[8,64,8,112]{3,2,1,0:T(8,128)(2,1)} reshape(bf16[512,896]{1,0:T(8,128)(2,1)} %fusion.9) | data formatting | bytes 1835008 | tf_op jit(solution)/shard_map/reshape | solution.py:33
  105.2 3.1 %reshape.181 = bf16[8,64,8,112]{3,2,1,0:T(8,128)(2,1)} reshape(bf16[512,896]{1,0:T(8,128)(2,1)} %convolution_convert_fusion.5) | data formatting | bytes 1835008 | tf_op jit(solution)/shard_map/reshape | solution.py:32
  108.3 1.4 collective-permute-start
  109.7 4.1 %fusion.48 = (f32[8,8,64]{2,1,0:T(8,128)S(1)}, f32[8,8,64,64]{2,3,1,0:T(8,128)}) fusion(pred[8,64,64]{1,2,0:T(8,128)(4,1)S(1)} %copy-done.6, bf16[8,64,8,112]{3,2,1,0:T(8,128)(2,1)} %reshape.181, bf16[8,64,8,112]{3,2,1,0:T(8,128)(2,1)} %reshape.180), kind=kOutput, calls=%fused_computation.91 | convolution fusion | flops 60031040 | bytes 2932736 | tf_op jit(solution)/shard_map/sub | solution.py:47
  113.9 2.5 fusion.12
  116.4 1.7 copy.59
  118.1 2.7 reshape.182
  120.8 3.8 %fusion.4 = bf16[512,1792]{1,0:T(8,128)(2,1)S(1)} fusion(bf16[512,1792]{1,0:T(8,128)(2,1)} %param.15, bf16[512,896]{1,0:T(8,128)(2,1)} %reshape.182, bf16[896,1792]{1,0:T(8,128)(2,1)S(1)} %copy-done), kind=kOutput, calls=%fused_computation.9 | convolution fusion | flops 1646919680 | bytes 7798784 | tf_op jit(solution)/shard_map/dot_general | solution.py:216
  124.7 0.0 copy-start.2
  124.7 0.7 fusion.5
  125.4 99.9 %all_to_all.27 = bf16[32,8,1792]{2,1,0:T(8,128)(2,1)} all-to-all(bf16[32,8,1792]{2,1,0:T(8,128)(2,1)S(1)} %fusion.5), channel_id=1, replica_groups=mesh['x'=2,'core'=2,'mp'=8] {'x','core','mp'}, dimensions={0} | all-to-all | bytes 1835008 | tf_op jit(solution)/shard_map/all_to_all | solution.py:227
  225.3 8.9 %all-gather.5.cloned.1.call-done.refs_4_ = bf16[896,3584]{1,0:T(8,128)(2,1)} async-done(((bf16[56,3584]{1,0:T(8,128)(2,1)}), bf16[896,3584]{1,0:T(8,128)(2,1)}) %all-gather.5.cloned.1.call-update) | async-done | bytes 6422544 | tf_op jit(solution)/shard_map/all_gather | solution.py:147
  234.2 0.5 collective-permute-start.1
  234.7 0.1 eq.86
  234.8 3.1 %fusion.6 = bf16[32,8,1792]{2,1,0:T(8,128)(2,1)} fusion(bf16[512,1792]{1,0:T(8,128)(2,1)} %copy-done.2, s32[256]{0:T(256)S(1)} %eq.86), kind=kOutput, calls=%fused_computation.13 | convolution fusion | flops 470351872 | bytes 2753536 | tf_op jit(solution)/shard_map/dot_general | solution.py:223
  237.9 3.4 %all-to-all-start.3 = ((bf16[32,8,1792]{2,1,0:T(8,128)(2,1)}), bf16[32,8,1792]{2,1,0:T(8,128)(2,1)}, u32[]{:S(2)}, u32[]{:S(2)}) async-start(bf16[32,8,1792]{2,1,0:T(8,128)(2,1)} %fusion.6), calls=%async_computation.3 | async-start | bytes 1835008 | tf_op jit(solution)/shard_map/all_to_all | solution.py:227
  241.3 0.1 pad_add_fusion.spots_ref
  241.4 24.6 %all-to-all-done.3 = bf16[32,8,1792]{2,1,0:T(8,128)(2,1)} async-done(((bf16[32,8,1792]{2,1,0:T(8,128)(2,1)}), bf16[32,8,1792]{2,1,0:T(8,128)(2,1)}, u32[]{:S(2)}, u32[]{:S(2)}) %all-to-all-start.3) | async-done | bytes 917536 | tf_op jit(solution)/shard_map/all_to_all | solution.py:227
  266.0 1.7 pad_maximum_fusion
  267.8 0.7 copy-done.1
  268.5 21.8 %gated_units.1 = bf16[512,3584]{1,0:T(8,128)(2,1)} custom-call(s32[8]{0:T(128)S(1)} %pad_add_fusion.spots_ref, bf16[512,1792]{1,0:T(8,128)(2,1)S(1)} %bitcast.38, f32[1,1792]{1,0:T(1,128)S(1)} %broadcast_in_dim.35.gain_ref, bf16[448,3584]{1,0:T(8,128)(2,1)S(1)} %copy-done.1, bf16[448,3584]{1,0:T(8,128)(2,1)} %collective-permute-done.refs_1_, ...), custom_call_target="tpu_custom_call" | custom-call | tf_op jit(solution)/shard_map/gated_units/pallas_call | solution.py:102
  (28 shorter events, 0.1 us)
Async XLA Ops:
  7.2 113.6 %copy-start = (bf16[896,1792]{1,0:T(8,128)(2,1)S(1)}, bf16[896,1792]{1,0:T(8,128)(2,1)}, u32[]{:S(2)}) copy-start(bf16[896,1792]{1,0:T(8,128)(2,1)} %param.20) | copy-start | bytes 9633796
  7.2 98.0 %all-gather.3.cloned.1.call-start = ((), (), s32[]{:S(2)}) async-start(), calls=%async_computation.4 | async-start | bytes 3612672 | tf_op jit(solution)/shard_map/all_gather | solution.py:146
  7.9 226.3 %all-gather.5.cloned.1.call-start = ((), (), s32[]{:S(2)}) async-start(), calls=%async_computation.5 | async-start | bytes 6823936 | tf_op jit(solution)/shard_map/all_gather | solution.py:147
  10.5 13.7 %all-to-all-start = ((bf16[8,1,4]{2,1,0:T(2,128)(2,1)}), bf16[8,1,4]{2,1,0:T(2,128)(2,1)S(1)}, u32[]{:S(2)}, u32[]{:S(2)}) async-start(bf16[8,1,4]{2,1,0:T(2,128)(2,1)} %copy.46), calls=%async_computation | async-start | bytes 8192 | tf_op jit(solution)/shard_map/all_to_all | solution.py:158
  27.1 5.1 %copy-start.11 = (s32[8]{0:T(128)S(1)}, s32[8]{0:T(128)}, u32[]{:S(2)}) copy-start(s32[8]{0:T(128)} %param.21) | copy-start | bytes 100
  27.1 8.1 %copy-start.7 = (f32[1792]{0:T(1024)S(1)}, f32[1792]{0:T(1024)}, u32[]{:S(2)}) copy-start(f32[1792]{0:T(1024)} %param.16) | copy-start | bytes 21508
  27.1 57.4 %all-to-all-start.1 = ((bf16[8,32,2688]{2,1,0:T(8,128)(2,1)}), bf16[8,32,2688]{2,1,0:T(8,128)(2,1)}, u32[]{:S(2)}, u32[]{:S(2)}) async-start(bf16[8,32,2688]{2,1,0:T(8,128)(2,1)} %copy.50), calls=%async_computation.1 | async-start | bytes 2752512 | tf_op jit(solution)/shard_map/all_to_all | solution.py:169
  32.2 3.0 %copy-start.3 = (bf16[512,1792]{1,0:T(8,128)(2,1)S(1)}, bf16[512,1792]{1,0:T(8,128)(2,1)}, u32[]{:S(2)}) copy-start(bf16[512,1792]{1,0:T(8,128)(2,1)} %param.15) | copy-start | bytes 5505028
  35.2 2.6 copy-start.9
  35.7 1.2 copy-start.4
  86.5 1.5 copy-start.5
  88.0 1.9 copy-start.10
  102.0 7.8 %copy-start.6 = (pred[8,64,64]{1,2,0:T(8,128)(4,1)S(1)}, pred[8,64,64]{1,2,0:T(8,128)(4,1)}, u32[]{:S(2)}) copy-start(pred[8,64,64]{1,2,0:T(8,128)(4,1)} %broadcast_and_fusion) | copy-start | bytes 98308
  108.3 117.0 %collective-permute-start = (bf16[448,3584]{1,0:T(8,128)(2,1)}, bf16[448,3584]{1,0:T(8,128)(2,1)}, u32[]{:S(2)}, u32[]{:S(2)}) collective-permute-start(bf16[448,3584]{1,0:T(8,128)(2,1)} %all-gather.3.cloned.1.call-done.refs_0_), channel_id=1, source_target_pairs={{0,16},{16,0},{1,17},{17,1},{2,18},{18,2},{3,19},{19,3},{4,20},{20... | collective-permute-start | bytes 9633800 | tf_op jit(solution)/shard_map/ppermute | solution.py:212
  124.7 100.6 %copy-start.2 = (bf16[512,1792]{1,0:T(8,128)(2,1)}, bf16[512,1792]{1,0:T(8,128)(2,1)S(1)}, u32[]{:S(2)}) copy-start(bf16[512,1792]{1,0:T(8,128)(2,1)S(1)} %fusion.4) | copy-start | bytes 5505028
  234.2 33.6 %collective-permute-start.3 = (bf16[896,3584]{1,0:T(8,128)(2,1)}, bf16[896,3584]{1,0:T(8,128)(2,1)}, u32[]{:S(2)}, u32[]{:S(2)}) collective-permute-start(bf16[896,3584]{1,0:T(8,128)(2,1)} %all-gather.5.cloned.1.call-done.refs_4_), channel_id=1, source_target_pairs={{0,8},{8,0},{1,9},{9,1},{2,10},{10,2},{3,11},{11,3},{4,12},{12,4},... | collective-permute-start | bytes 19267592 | tf_op jit(solution)/shard_map/ppermute | solution.py:231
  234.2 33.6 %collective-permute-start.1 = (bf16[448,3584]{1,0:T(8,128)(2,1)}, bf16[448,3584]{1,0:T(8,128)(2,1)}, u32[]{:S(2)}, u32[]{:S(2)}) collective-permute-start(bf16[448,3584]{1,0:T(8,128)(2,1)} %all-gather.3.cloned.1.call-done.refs_0_), channel_id=1, source_target_pairs={{0,8},{8,0},{1,9},{9,1},{2,10},{10,2},{3,11},{11,3},{4,12},{12,4},... | collective-permute-start | bytes 9633800 | tf_op jit(solution)/shard_map/ppermute | solution.py:230
  234.7 33.1 %collective-permute-start.2 = (bf16[448,3584]{1,0:T(8,128)(2,1)}, bf16[448,3584]{1,0:T(8,128)(2,1)}, u32[]{:S(2)}, u32[]{:S(2)}) collective-permute-start(bf16[448,3584]{1,0:T(8,128)(2,1)} %collective-permute-done.refs_1_), channel_id=1, source_target_pairs={{0,8},{8,0},{1,9},{9,1},{2,10},{10,2},{3,11},{11,3},{4,12},{12,4},... | collective-permute-start | bytes 9633800 | tf_op jit(solution)/shard_map/ppermute | solution.py:230
  234.8 6.5 %copy-start.8 = (f32[1792]{0:T(1024)S(1)}, f32[1792]{0:T(1024)}, u32[]{:S(2)}) copy-start(f32[1792]{0:T(1024)} %param.27) | copy-start | bytes 21508
  237.9 28.1 %all-to-all-start.3 = ((bf16[32,8,1792]{2,1,0:T(8,128)(2,1)}), bf16[32,8,1792]{2,1,0:T(8,128)(2,1)}, u32[]{:S(2)}, u32[]{:S(2)}) async-start(bf16[32,8,1792]{2,1,0:T(8,128)(2,1)} %fusion.6), calls=%async_computation.3 | async-start | bytes 1835008 | tf_op jit(solution)/shard_map/all_to_all | solution.py:227
  266.0 2.5 copy-start.1
Sparse Core Ops, SparseCore 0:
  10.2 83.6 all-gather.2
  96.6 137.5 all-gather.4

commit v3 on v1

--- a/solution.py
+++ b/solution.py
@@ -55,31 +55,67 @@
 CORES = 2
 
 
-def gated_kernel(own_ref, sib_ref, go_ref, gs_ref, uo_ref, us_ref, o_ref):
-    own = own_ref[...]
-    sib = sib_ref[...]
-    gate = jnp.dot(own, go_ref[...], preferred_element_type=jnp.float32)
-    gate += jnp.dot(sib, gs_ref[...], preferred_element_type=jnp.float32)
-    up = jnp.dot(own, uo_ref[...], preferred_element_type=jnp.float32)
-    up += jnp.dot(sib, us_ref[...], preferred_element_type=jnp.float32)
-    o_ref[...] = (gate * jax.nn.sigmoid(gate) * up).astype(o_ref.dtype)
-
-
-def gated(own, sib, gate_own, gate_sib, up_own, up_sib):
-    rows, depth = own.shape
-    width = gate_own.shape[1]
+def gate_kernel(rows_ref, gain_ref, w_ref, act_ref, o_ref):
+    @pl.when(pl.program_id(0) == 0)
+    def _():
+        @pl.loop(0, rows_ref.shape[0], step=64)
+        def _(r):
+            part = pl.ds(pl.multiple_of(r, 64), 64)
+            wide = rows_ref[part, :].astype(jnp.float32)
+            scale = lax.rsqrt(jnp.mean(wide * wide, axis=-1, keepdims=True) + EPSILON)
+            act_ref[part, :] = (wide * scale * gain_ref[...]).astype(jnp.bfloat16)
+
+    gate = jnp.dot(act_ref[...], w_ref[...], preferred_element_type=jnp.float32)
+    o_ref[...] = gate * jax.nn.sigmoid(gate)
+
+
+def gate_units(regrouped, gain, weight):
+    rows, depth = regrouped.shape
+    width = weight.shape[1]
     tile = 512
-    act = pl.BlockSpec((rows, depth), lambda i: (0, 0))
-    wgt = pl.BlockSpec((depth, tile), lambda i: (0, i))
+    whole = lambda i: (0, 0)
+    strip = lambda i: (0, i)
     return pl.pallas_call(
-        gated_kernel,
+        gate_kernel,
+        out_shape=(
+            jax.ShapeDtypeStruct((rows, depth), jnp.bfloat16),
+            jax.ShapeDtypeStruct((rows, width), jnp.float32),
+        ),
+        grid=(width // tile,),
+        in_specs=[
+            pl.BlockSpec((rows, depth), whole),
+            pl.BlockSpec((1, depth), whole),
+            pl.BlockSpec((depth, tile), strip),
+        ],
+        out_specs=(pl.BlockSpec((rows, depth), whole), pl.BlockSpec((rows, tile), strip)),
+        compiler_params=pltpu.CompilerParams(vmem_limit_bytes=32 << 20),
+        name="gate_units",
+    )(regrouped, gain[None, :], weight)
+
+
+def up_kernel(act_ref, silu_ref, w_ref, o_ref):
+    up = jnp.dot(act_ref[...], w_ref[...], preferred_element_type=jnp.float32)
+    o_ref[...] = (silu_ref[...] * up).astype(o_ref.dtype)
+
+
+def up_units(act, silu, weight):
+    rows, depth = act.shape
+    width = weight.shape[1]
+    tile = 512
+    strip = lambda i: (0, i)
+    return pl.pallas_call(
+        up_kernel,
         out_shape=jax.ShapeDtypeStruct((rows, width), jnp.bfloat16),
         grid=(width // tile,),
-        in_specs=[act, act, wgt, wgt, wgt, wgt],
-        out_specs=pl.BlockSpec((rows, tile), lambda i: (0, i)),
-        compiler_params=pltpu.CompilerParams(vmem_limit_bytes=40 << 20),
-        name="gated_units",
-    )(own, sib, gate_own, gate_sib, up_own, up_sib)
+        in_specs=[
+            pl.BlockSpec((rows, depth), lambda i: (0, 0)),
+            pl.BlockSpec((rows, tile), strip),
+            pl.BlockSpec((depth, tile), strip),
+        ],
+        out_specs=pl.BlockSpec((rows, tile), strip),
+        compiler_params=pltpu.CompilerParams(vmem_limit_bytes=48 << 20),
+        name="up_units",
+    )(act, silu, weight)
 
 
 def local(
@@ -104,13 +140,9 @@
     tok_dev = tokens.shape[0]
     hw_size = query_weight.shape[1]
     every = ("x", "core", "mp")
-    swap = [(0, 1), (1, 0)]
-    core = lax.axis_index("core")
-
-    gate_own = lax.all_gather(gate_weight, ("x", "mp"), axis=0, tiled=True)
-    up_own = lax.all_gather(up_weight, ("x", "mp"), axis=0, tiled=True)
-    gate_sib = lax.ppermute(gate_own, "core", swap)
-    up_sib = lax.ppermute(up_own, "core", swap)
+
+    gate_full = lax.all_gather(gate_weight, every, axis=0, tiled=True)
+    up_full = lax.all_gather(up_weight, every, axis=0, tiled=True)
 
     matches = (slot_adapter_ids[None, :] == request_adapter[:, None]).astype(jnp.int32)
     slot_ids = jnp.sum(
@@ -177,16 +209,13 @@
         tokens.astype(jnp.float32)
         + jnp.dot(attended, output_weight, preferred_element_type=jnp.float32)
     ).astype(jnp.bfloat16)
-    order = (device_token_order[0][:, None] == jnp.arange(tok_dev)[None, :]).astype(jnp.bfloat16)
-    shuffled = jnp.dot(order, residual, preferred_element_type=jnp.float32).astype(jnp.bfloat16)
+    order = device_token_order.reshape(-1, 1) == jnp.arange(tok_dev)[None, :]
+    shuffled = jnp.dot(
+        order.astype(jnp.bfloat16), residual, preferred_element_type=jnp.float32
+    ).astype(jnp.bfloat16)
     regrouped = lax.all_to_all(shuffled, every, split_axis=0, concat_axis=0, tiled=True)
-    mlp_input = normalize(regrouped, second_norm_gain)
-    by_core = mlp_input.reshape(tok_dev, lax.axis_size("x"), CORES, -1)
-    even = by_core[:, :, 0].reshape(tok_dev, -1)
-    odd = by_core[:, :, 1].reshape(tok_dev, -1)
-    own = jnp.where(core == 0, even, odd)
-    sib = jnp.where(core == 0, odd, even)
-    hidden = gated(own, sib, gate_own, gate_sib, up_own, up_sib)
+    act, silu = gate_units(regrouped, second_norm_gain, gate_full)
+    hidden = up_units(act, silu, up_full)
     return (residual, hidden)
 
 

time: 334 us -> 264 us (0.79)
  waiting for transfers between devices: 195 us -> 143 us
  local copies, waits for them, and re-layouts: 42 us -> 28.8 us
  other arithmetic: 15.1 us -> 4.34 us
  Pallas kernels: 19.6 us -> 26 us
    all_gather x2, waiting for transfers between devices: 107 us -> 44.8 us  [the longest x1 44.8 us: local(): up_full = lax.all_gather(up_weight, every, axis=0, tiled=True)]
    all_to_all x1, waiting for transfers between devices: 44.4 us -> 55.4 us  [local(): lax.all_to_all(shuffled, every, split_axis=0, concat_axis=0, tiled=True)]
    select_n x4 -> x0, local copies, waits for them, and re-layouts: 9.13 us -> none  [the longest x2 6.13 us: local(): sib = jnp.where(core == 0, odd, even)]
    pallas_call x1 -> x2, Pallas kernels: 19.6 us -> 26 us  [the longest x1 13.3 us: up_units(): pl.pallas_call(up_kernel, out_shape=jax.ShapeDtypeStruct((rows, width), j...]
    select_n x1 -> x0, other arithmetic: 5.92 us -> none  [local(): sib = jnp.where(core == 0, odd, even)]
    convert_element_type x1 -> x0, local copies, waits for them, and re-layouts: 5.54 us -> none  [normalize(): floated = rows_in.astype(jnp.float32)]
    convert_element_type x2 -> x1, other arithmetic: 4.9 us -> 0.49 us  [normalize(): return (floated * scale * gain_vec).astype(jnp.bfloat16)]
  transfers between devices with their start and end apart: 7 -> 5, of which waited for: 5 -> 4; matrix products, arithmetic and copies ran while one was open for 25% -> 20% of each run, Pallas kernels for 0% -> 5%
where the time goes in v3:
time: 264 us; the launch traced here: 263 us
  waiting for transfers between devices  143 us (54%)
  matrix products  30 us (11%)
  local copies, waits for them, and re-layouts  28.8 us (11%)
  Pallas kernels  26 us (10%)
  starting transfers between devices  16.5 us (6%)
  between operations  14.3 us (5%)
  other arithmetic  4.34 us (2%)
    all_to_all x1, waiting for transfers between devices, local(): lax.all_to_all(shuffled, every, split_axis=0, concat_axis=0, tiled=True)  55.4 us
    all_gather x1, waiting for transfers between devices, local(): up_full = lax.all_gather(up_weight, every, axis=0, tiled=True)  44.8 us
    all_to_all x1, waiting for transfers between devices, local(): lax.all_to_all(outgoing, 'mp', split_axis=0, concat_axis=0, tiled=True)  38.4 us
    pallas_call x1, Pallas kernels, up_units(): pl.pallas_call(up_kernel, out_shape=jax.ShapeDtypeStruct((rows, width), j...  13.3 us
    unnamed x34, local copies, waits for them, and re-layouts  12.9 us
    pallas_call x1, Pallas kernels, gate_units(): pl.pallas_call(gate_kernel, out_shape=(jax.ShapeDtypeStruct((rows, depth)...  12.7 us
    all_to_all x1, starting transfers between devices, local(): lax.all_to_all(chosen, 'mp', split_axis=0, concat_axis=0, tiled=True)  7.28 us
    dot_general x1, matrix products, local(): jnp.dot(normed, value_weight, preferred_element_type=jnp.float32)  5.51 us
  transfers between devices with their start and end apart: 5, of which 4 were waited for; matrix products, arithmetic and copies ran while one was open for 20% of the time, Pallas kernels for 5%

profile of v3, /device:TPU:0, one launch (start us, length us, event | category | flops | bytes accessed | tf_op | source)
XLA Modules:
  0.0 263.4 jit_solution(2731226896228758337)
XLA Ops:
  7.2 0.0 copy-start
  7.2 0.0 copy-start.7
  7.2 0.0 all-gather.3.cloned.1.call-start
  7.2 0.7 all-gather.3.cloned.1.call-update
  7.9 0.0 all-gather.5.cloned.1.call-start
  8.0 0.7 all-gather.5.cloned.1.call-update
  8.7 0.9 select_reduce_fusion
  9.5 0.3 fusion.11
  9.8 0.7 copy.46
  10.5 7.3 %all-to-all-start = ((bf16[8,1,4]{2,1,0:T(2,128)(2,1)}), bf16[8,1,4]{2,1,0:T(2,128)(2,1)S(1)}, u32[]{:S(2)}, u32[]{:S(2)}) async-start(bf16[8,1,4]{2,1,0:T(2,128)(2,1)} %copy.46), calls=%async_computation | async-start | bytes 8192 | tf_op jit(solution)/shard_map/all_to_all | solution.py:156
  17.8 2.1 copy.84
  19.9 0.0 copy-done.7
  19.9 0.8 copy.49
  20.7 3.5 %all-to-all-done = bf16[8,1,4]{2,1,0:T(2,128)(2,1)S(1)} async-done(((bf16[8,1,4]{2,1,0:T(2,128)(2,1)}), bf16[8,1,4]{2,1,0:T(2,128)(2,1)S(1)}, u32[]{:S(2)}, u32[]{:S(2)}) %all-to-all-start) | async-done | bytes 96 | tf_op jit(solution)/shard_map/all_to_all | solution.py:156
  24.2 0.1 copy.47
  24.3 1.7 convolution_convert_fusion.1
  26.1 1.2 copy.50
  27.3 4.4 %all-to-all-start.1 = ((bf16[8,32,2688]{2,1,0:T(8,128)(2,1)}), bf16[8,32,2688]{2,1,0:T(8,128)(2,1)}, u32[]{:S(2)}, u32[]{:S(2)}) async-start(bf16[8,32,2688]{2,1,0:T(8,128)(2,1)} %copy.50), calls=%async_computation.1 | async-start | bytes 2752512 | tf_op jit(solution)/shard_map/all_to_all | solution.py:167
  31.7 0.0 copy-start.4
  31.7 2.1 fusion.1
  33.8 0.0 copy-done.9
  33.8 0.0 copy-done.4
  33.8 0.0 copy-start.11
  33.8 0.5 fusion.3
  34.3 0.0 copy-start.5
  34.3 1.2 copy-done.5
  35.6 0.8 copy-done.11
  36.4 3.0 %convolution_convert_fusion.4 = bf16[512,896]{1,0:T(8,128)(2,1)} fusion(bf16[512,1792]{1,0:T(8,128)(2,1)S(1)} %fusion.3, bf16[1792,896]{1,0:T(8,128)(2,1)S(1)} %copy-done.11), kind=kOutput, calls=%fused_computation.22 | convolution fusion | flops 1644625920 | bytes 5963776 | tf_op jit(solution)/shard_map/dot_general | solution.py:202
  39.4 3.1 %reshape.169 = bf16[8,64,8,112]{3,2,1,0:T(8,128)(2,1)} reshape(bf16[512,896]{1,0:T(8,128)(2,1)} %convolution_convert_fusion.4) | data formatting | bytes 1835008 | tf_op jit(solution)/shard_map/reshape | solution.py:30
  42.6 0.0 copy-done.14
  42.6 0.1 iota_compare_fusion.6
  42.6 0.1 fusion.29
  42.7 0.8 broadcast_and_fusion
  43.5 38.4 %all-to-all-done.1 = bf16[8,32,2688]{2,1,0:T(8,128)(2,1)} async-done(((bf16[8,32,2688]{2,1,0:T(8,128)(2,1)}), bf16[8,32,2688]{2,1,0:T(8,128)(2,1)}, u32[]{:S(2)}, u32[]{:S(2)}) %all-to-all-start.1) | async-done | bytes 1376288 | tf_op jit(solution)/shard_map/all_to_all | solution.py:167
  81.8 2.0 convolution_convert_fusion
  83.8 0.0 copy-start.6
  83.8 0.1 slice.20
  83.9 1.4 copy-done.6
  85.3 0.6 convolution_convert_fusion.5
  85.9 0.5 multiply_convert_fusion
  86.4 0.8 copy-done.12
  87.2 3.0 %fusion.6 = bf16[512,896]{1,0:T(8,128)(2,1)} fusion(bf16[512,896]{1,0:T(8,128)(2,1)S(1)} %bitcast.38, bf16[512,1792]{1,0:T(8,128)(2,1)S(1)} %copy-done.6, bf16[1792,896]{1,0:T(8,128)(2,1)S(1)} %copy-done.12), kind=kOutput, calls=%fused_computation.16 | convolution fusion | flops 1645543424 | bytes 6881280 | tf_op jit(solution)/shard_map/dot_general | solution.py:199
  90.2 3.1 %reshape.168 = bf16[8,64,8,112]{3,2,1,0:T(8,128)(2,1)} reshape(bf16[512,896]{1,0:T(8,128)(2,1)} %fusion.6) | data formatting | bytes 1835008 | tf_op jit(solution)/shard_map/reshape | solution.py:29
  93.3 0.4 multiply_convert_fusion.1
  93.8 5.5 %fusion.7 = bf16[512,896]{1,0:T(8,128)(2,1)} fusion(bf16[512,896]{1,0:T(8,128)(2,1)S(1)} %bitcast.37, bf16[512,1792]{1,0:T(8,128)(2,1)} %copy-done.5, bf16[1792,896]{1,0:T(8,128)(2,1)} %param.19), kind=kOutput, calls=%fused_computation.18 | convolution fusion | flops 1645543424 | bytes 6881280 | tf_op jit(solution)/shard_map/dot_general | solution.py:204
  99.3 3.2 %reshape.167 = bf16[8,64,8,112]{3,2,1,0:T(8,128)(2,1)} reshape(bf16[512,896]{1,0:T(8,128)(2,1)} %fusion.7) | data formatting | bytes 1835008 | tf_op jit(solution)/shard_map/reshape | solution.py:31
  102.5 0.0 copy-done.8
  102.5 4.1 %fusion.41 = (f32[8,8,64]{2,1,0:T(8,128)S(1)}, f32[8,8,64,64]{2,3,1,0:T(8,128)}) fusion(pred[8,64,64]{1,2,0:T(8,128)(4,1)S(1)} %copy-done.8, bf16[8,64,8,112]{3,2,1,0:T(8,128)(2,1)} %reshape.169, bf16[8,64,8,112]{3,2,1,0:T(8,128)(2,1)} %reshape.168), kind=kOutput, calls=%fused_computation.73 | convolution fusion | flops 60031040 | bytes 2932736 | tf_op jit(solution)/shard_map/sub | solution.py:45
  106.6 2.5 fusion.10
  109.1 1.7 copy.59
  110.8 2.7 %reshape.170 = bf16[512,896]{1,0:T(8,128)(2,1)} reshape(bf16[8,64,8,112]{3,2,1,0:T(8,128)(2,1)} %copy.59) | data formatting | bytes 1835008 | tf_op jit(solution)/shard_map/reshape | solution.py:52
  113.5 0.0 copy-done
  113.5 4.0 %fusion.4 = bf16[512,1792]{1,0:T(8,128)(2,1)S(1)} fusion(bf16[512,1792]{1,0:T(8,128)(2,1)} %param.15, bf16[512,896]{1,0:T(8,128)(2,1)} %reshape.170, bf16[896,1792]{1,0:T(8,128)(2,1)S(1)} %copy-done), kind=kOutput, calls=%fused_computation.9 | convolution fusion | flops 1646919680 | bytes 7798784 | tf_op jit(solution)/shard_map/dot_general | solution.py:210
  117.5 0.0 copy-start.15
  117.5 0.0 copy-done.13
  117.6 2.4 convolution_convert_fusion.2
  120.0 4.7 %all-to-all-start.2 = ((bf16[32,16,1792]{2,1,0:T(8,128)(2,1)}), bf16[32,16,1792]{2,1,0:T(8,128)(2,1)}, u32[]{:S(2)}, u32[]{:S(2)}) async-start(bf16[32,16,1792]{2,1,0:T(8,128)(2,1)} %bitcast.36), calls=%async_computation.2 | async-start | bytes 3670016 | tf_op jit(solution)/shard_map/all_to_all | solution.py:216
  124.7 55.4 %all-to-all-done.2 = bf16[32,16,1792]{2,1,0:T(8,128)(2,1)} async-done(((bf16[32,16,1792]{2,1,0:T(8,128)(2,1)}), bf16[32,16,1792]{2,1,0:T(8,128)(2,1)}, u32[]{:S(2)}, u32[]{:S(2)}) %all-to-all-start.2) | async-done | bytes 1835040 | tf_op jit(solution)/shard_map/all_to_all | solution.py:216
  180.2 12.7 %gate_units.1 = (bf16[512,1792]{1,0:T(8,128)(2,1)S(1)}, f32[512,3584]{1,0:T(8,128)S(1)}) custom-call(bf16[512,1792]{1,0:T(8,128)(2,1)} %bitcast.12.rows_ref, f32[1,1792]{1,0:T(1,128)S(1)} %broadcast_in_dim.35.gain_ref, bf16[1792,3584]{1,0:T(8,128)(2,1)} %all-gather.3.cloned.1.call-done.w_ref), custom_call_target="tpu_custom_call" | custom-call | tf_op jit(solution)/shard_map/gate_units/pallas_call | solution.py:78
  192.9 2.9 %copy-done.1 = f32[512,3584]{1,0:T(8,128)} copy-done((f32[512,3584]{1,0:T(8,128)}, f32[512,3584]{1,0:T(8,128)S(1)}, u32[]{:S(2)}) %copy-start.1) | copy-done | bytes 7340056
  195.8 1.2 copy-done.2
  197.0 44.8 %all-gather.5.cloned.1.call-done.w_ref = bf16[1792,3584]{1,0:T(8,128)(2,1)} async-done(((bf16[56,3584]{1,0:T(8,128)(2,1)}), bf16[1792,3584]{1,0:T(8,128)(2,1)}) %all-gather.5.cloned.1.call-update) | async-done | bytes 12845072 | tf_op jit(solution)/shard_map/all_gather | solution.py:145
  241.8 1.5 copy-done.3
  243.3 13.3 %up_units.1 = bf16[512,3584]{1,0:T(8,128)(2,1)} custom-call(bf16[512,1792]{1,0:T(8,128)(2,1)S(1)} %copy-done.3, f32[512,3584]{1,0:T(8,128)} %copy-done.1, bf16[1792,3584]{1,0:T(8,128)(2,1)} %all-gather.5.cloned.1.call-done.w_ref), custom_call_target="tpu_custom_call" | custom-call | tf_op jit(solution)/shard_map/up_units/pallas_call | solution.py:106
  (17 shorter events, 0.1 us)
Async XLA Ops:
  7.2 106.3 %copy-start = (bf16[896,1792]{1,0:T(8,128)(2,1)S(1)}, bf16[896,1792]{1,0:T(8,128)(2,1)}, u32[]{:S(2)}) copy-start(bf16[896,1792]{1,0:T(8,128)(2,1)} %param.20) | copy-start | bytes 9633796
  7.2 12.7 %copy-start.7 = (bf16[4,2,16,896]{3,2,1,0:T(8,128)(2,1)S(1)}, bf16[4,2,16,896]{3,2,1,0:T(8,128)(2,1)}, u32[]{:S(2)}) copy-start(bf16[4,2,16,896]{3,2,1,0:T(8,128)(2,1)} %param.25) | copy-start | bytes 688132
  7.2 173.0 %all-gather.3.cloned.1.call-start = ((), (), s32[]{:S(2)}) async-start(), calls=%async_computation.3 | async-start | bytes 13246464 | tf_op jit(solution)/shard_map/all_gather | solution.py:144
  7.9 233.9 %all-gather.5.cloned.1.call-start = ((), (), s32[]{:S(2)}) async-start(), calls=%async_computation.4 | async-start | bytes 13246464 | tf_op jit(solution)/shard_map/all_gather | solution.py:145
  10.5 13.7 %all-to-all-start = ((bf16[8,1,4]{2,1,0:T(2,128)(2,1)}), bf16[8,1,4]{2,1,0:T(2,128)(2,1)S(1)}, u32[]{:S(2)}, u32[]{:S(2)}) async-start(bf16[8,1,4]{2,1,0:T(2,128)(2,1)} %copy.46), calls=%async_computation | async-start | bytes 8192 | tf_op jit(solution)/shard_map/all_to_all | solution.py:156
  27.3 6.5 %copy-start.9 = (f32[1792]{0:T(1024)S(1)}, f32[1792]{0:T(1024)}, u32[]{:S(2)}) copy-start(f32[1792]{0:T(1024)} %param.16) | copy-start | bytes 21508
  27.3 54.5 %all-to-all-start.1 = ((bf16[8,32,2688]{2,1,0:T(8,128)(2,1)}), bf16[8,32,2688]{2,1,0:T(8,128)(2,1)}, u32[]{:S(2)}, u32[]{:S(2)}) async-start(bf16[8,32,2688]{2,1,0:T(8,128)(2,1)} %copy.50), calls=%async_computation.1 | async-start | bytes 2752512 | tf_op jit(solution)/shard_map/all_to_all | solution.py:167
  31.7 2.1 copy-start.4
  33.8 2.6 copy-start.11
  34.3 1.2 copy-start.5
  39.4 3.1 %copy-start.14 = (s32[8]{0:T(128)S(1)}, s32[8]{0:T(128)}, u32[]{:S(2)}) copy-start(s32[8]{0:T(128)} %param.21) | copy-start | bytes 100
  83.8 1.5 copy-start.6
  85.3 1.9 copy-start.12
  99.3 3.2 %copy-start.8 = (pred[8,64,64]{1,2,0:T(8,128)(4,1)S(1)}, pred[8,64,64]{1,2,0:T(8,128)(4,1)}, u32[]{:S(2)}) copy-start(pred[8,64,64]{1,2,0:T(8,128)(4,1)} %broadcast_and_fusion) | copy-start | bytes 98308
  113.5 4.1 %copy-start.13 = (s32[1,512]{1,0:T(1,128)S(1)}, s32[1,512]{1,0:T(1,128)}, u32[]{:S(2)}) copy-start(s32[1,512]{1,0:T(1,128)} %param.26) | copy-start | bytes 6148
  117.5 2.4 copy-start.15
  120.0 4.7 %copy-start.10 = (f32[1792]{0:T(1024)S(1)}, f32[1792]{0:T(1024)}, u32[]{:S(2)}) copy-start(f32[1792]{0:T(1024)} %param.27) | copy-start | bytes 21508
  120.0 60.2 %all-to-all-start.2 = ((bf16[32,16,1792]{2,1,0:T(8,128)(2,1)}), bf16[32,16,1792]{2,1,0:T(8,128)(2,1)}, u32[]{:S(2)}, u32[]{:S(2)}) async-start(bf16[32,16,1792]{2,1,0:T(8,128)(2,1)} %bitcast.36), calls=%async_computation.2 | async-start | bytes 3670016 | tf_op jit(solution)/shard_map/all_to_all | solution.py:216
  192.9 2.9 %copy-start.1 = (f32[512,3584]{1,0:T(8,128)}, f32[512,3584]{1,0:T(8,128)S(1)}, u32[]{:S(2)}) copy-start(f32[512,3584]{1,0:T(8,128)S(1)} %get-tuple-element.5.silu_ref) | copy-start | bytes 22020100
  195.8 1.2 copy-start.2
  241.8 1.5 copy-start.3
Sparse Core Ops, SparseCore 0:
  10.9 118.8 all-gather.2
  132.8 108.9 all-gather.4

commit v4 on v3

--- a/solution.py
+++ b/solution.py
@@ -93,29 +93,31 @@
     )(regrouped, gain[None, :], weight)
 
 
-def up_kernel(act_ref, silu_ref, w_ref, o_ref):
+def up_kernel(act_ref, silu_ref, w_ref, *refs):
     up = jnp.dot(act_ref[...], w_ref[...], preferred_element_type=jnp.float32)
-    o_ref[...] = (silu_ref[...] * up).astype(o_ref.dtype)
-
-
-def up_units(act, silu, weight):
+    refs[-1][...] = (silu_ref[...] * up).astype(refs[-1].dtype)
+
+
+def up_units(act, silu, weight, first, earlier=None):
     rows, depth = act.shape
-    width = weight.shape[1]
     tile = 512
-    strip = lambda i: (0, i)
+    strip = lambda i: (0, i + first // tile)
+    given = [] if earlier is None else [earlier]
     return pl.pallas_call(
         up_kernel,
-        out_shape=jax.ShapeDtypeStruct((rows, width), jnp.bfloat16),
-        grid=(width // tile,),
+        out_shape=jax.ShapeDtypeStruct(silu.shape, jnp.bfloat16),
+        grid=(weight.shape[1] // tile,),
         in_specs=[
             pl.BlockSpec((rows, depth), lambda i: (0, 0)),
             pl.BlockSpec((rows, tile), strip),
-            pl.BlockSpec((depth, tile), strip),
-        ],
+            pl.BlockSpec((depth, tile), lambda i: (0, i)),
+        ]
+        + [pl.BlockSpec(memory_space=pl.ANY) for _ in given],
         out_specs=pl.BlockSpec((rows, tile), strip),
+        input_output_aliases={3: 0} if given else {},
         compiler_params=pltpu.CompilerParams(vmem_limit_bytes=48 << 20),
         name="up_units",
-    )(act, silu, weight)
+    )(act, silu, weight, *given)
 
 
 def local(
@@ -142,7 +144,9 @@
     every = ("x", "core", "mp")
 
     gate_full = lax.all_gather(gate_weight, every, axis=0, tiled=True)
-    up_full = lax.all_gather(up_weight, every, axis=0, tiled=True)
+    early = up_weight.shape[1] * 5 // 7
+    up_early = lax.all_gather(up_weight[:, :early], every, axis=0, tiled=True)
+    up_late = lax.all_gather(up_weight[:, early:], every, axis=0, tiled=True)
 
     matches = (slot_adapter_ids[None, :] == request_adapter[:, None]).astype(jnp.int32)
     slot_ids = jnp.sum(
@@ -215,7 +219,8 @@
     ).astype(jnp.bfloat16)
     regrouped = lax.all_to_all(shuffled, every, split_axis=0, concat_axis=0, tiled=True)
     act, silu = gate_units(regrouped, second_norm_gain, gate_full)
-    hidden = up_units(act, silu, up_full)
+    hidden = up_units(act, silu, up_early, 0)
+    hidden = up_units(act, silu, up_late, early, hidden)
     return (residual, hidden)
 
 

time: 264 us -> 301 us (1.14)
  waiting for transfers between devices: 143 us -> 175 us
  local copies, waits for them, and re-layouts: 28.8 us -> 34.5 us
    all_gather x1 -> x2, waiting for transfers between devices: 44.8 us -> 83 us  [the longest x1 50.5 us: local(): up_late = lax.all_gather(up_weight[:, early:], every, axis=0, tiled=True)]
    all_to_all x1, waiting for transfers between devices: 55.4 us -> 50.9 us  [local(): lax.all_to_all(shuffled, every, split_axis=0, concat_axis=0, tiled=True)]
    slice x0 -> x2, local copies, waits for them, and re-layouts: none -> 3.37 us  [the longest x1 1.81 us: local(): up_early = lax.all_gather(up_weight[:, :early], every, axis=0, tiled=True)]
    unnamed x34 -> x40, local copies, waits for them, and re-layouts: 12.9 us -> 15.2 us
    pallas_call x1 -> x2, Pallas kernels: 13.3 us -> 14.5 us  [up_units(): pl.pallas_call(up_kernel, out_shape=jax.ShapeDtypeStruct(silu.shape, jnp....]
  transfers between devices with their start and end apart: 5 -> 6, of which waited for: 4 -> 5; matrix products, arithmetic and copies ran while one was open for 20% -> 19% of each run, Pallas kernels for 5% -> 7%
where the time goes in v4:
time: 301 us; the launch traced here: 300 us
  waiting for transfers between devices  175 us (58%)
  local copies, waits for them, and re-layouts  34.5 us (11%)
  matrix products  30.3 us (10%)
  Pallas kernels  26.6 us (9%)
  starting transfers between devices  16 us (5%)
  between operations  14 us (5%)
  other arithmetic  4.35 us (1%)
    all_to_all x1, waiting for transfers between devices, local(): lax.all_to_all(shuffled, every, split_axis=0, concat_axis=0, tiled=True)  50.9 us
    all_gather x1, waiting for transfers between devices, local(): up_late = lax.all_gather(up_weight[:, early:], every, axis=0, tiled=True)  50.5 us
    all_to_all x1, waiting for transfers between devices, local(): lax.all_to_all(outgoing, 'mp', split_axis=0, concat_axis=0, tiled=True)  36.3 us
    all_gather x1, waiting for transfers between devices, local(): up_early = lax.all_gather(up_weight[:, :early], every, axis=0, tiled=True)  32.5 us
    unnamed x40, local copies, waits for them, and re-layouts  15.2 us
    pallas_call x2, Pallas kernels, up_units(): pl.pallas_call(up_kernel, out_shape=jax.ShapeDtypeStruct(silu.shape, jnp....  14.5 us
    pallas_call x1, Pallas kernels, gate_units(): pl.pallas_call(gate_kernel, out_shape=(jax.ShapeDtypeStruct((rows, depth)...  12.1 us
    all_to_all x1, starting transfers between devices, local(): lax.all_to_all(chosen, 'mp', split_axis=0, concat_axis=0, tiled=True)  7.28 us
  transfers between devices with their start and end apart: 6, of which 5 were waited for; matrix products, arithmetic and copies ran while one was open for 19% of the time, Pallas kernels for 7%

profile of v4, /device:TPU:0, one launch (start us, length us, event | category | flops | bytes accessed | tf_op | source)
XLA Modules:
  0.0 300.2 jit_solution(9422849066531543182)
XLA Ops:
  7.2 0.0 copy-start
  7.2 0.0 all-gather.4.cloned.1.call-start
  7.2 0.7 all-gather.4.cloned.1.call-update
  7.9 0.0 all-gather.8.cloned.1.call-start
  8.0 1.8 slice.27
  9.8 0.0 all-gather.8.cloned.1.call-update
  9.8 0.9 select_reduce_fusion
  10.7 0.3 fusion.11
  10.9 0.7 copy.47
  11.6 7.3 %all-to-all-start = ((bf16[8,1,4]{2,1,0:T(2,128)(2,1)}), bf16[8,1,4]{2,1,0:T(2,128)(2,1)S(1)}, u32[]{:S(2)}, u32[]{:S(2)}) async-start(bf16[8,1,4]{2,1,0:T(2,128)(2,1)} %copy.47), calls=%async_computation | async-start | bytes 8192 | tf_op jit(solution)/shard_map/all_to_all | solution.py:160
  18.9 2.1 copy.85
  21.0 0.0 copy-done.10
  21.0 0.8 copy.50
  21.9 3.5 %all-to-all-done = bf16[8,1,4]{2,1,0:T(2,128)(2,1)S(1)} async-done(((bf16[8,1,4]{2,1,0:T(2,128)(2,1)}), bf16[8,1,4]{2,1,0:T(2,128)(2,1)S(1)}, u32[]{:S(2)}, u32[]{:S(2)}) %all-to-all-start) | async-done | bytes 96 | tf_op jit(solution)/shard_map/all_to_all | solution.py:160
  25.4 0.1 copy.48
  25.5 1.7 convolution_convert_fusion.1
  27.2 1.2 copy.51
  28.4 4.4 %all-to-all-start.1 = ((bf16[8,32,2688]{2,1,0:T(8,128)(2,1)}), bf16[8,32,2688]{2,1,0:T(8,128)(2,1)}, u32[]{:S(2)}, u32[]{:S(2)}) async-start(bf16[8,32,2688]{2,1,0:T(8,128)(2,1)} %copy.51), calls=%async_computation.1 | async-start | bytes 2752512 | tf_op jit(solution)/shard_map/all_to_all | solution.py:171
  32.8 0.0 all-gather.6.cloned.1.call-start
  32.9 1.6 slice.26
  34.4 0.0 all-gather.6.cloned.1.call-update
  34.5 0.0 copy-start.7
  34.5 2.1 fusion.1
  36.6 0.0 copy-start.14
  36.6 0.5 fusion.3
  37.1 0.0 copy-start.8
  37.1 1.2 copy-done.8
  38.3 0.8 copy-done.14
  39.1 3.0 %convolution_convert_fusion.4 = bf16[512,896]{1,0:T(8,128)(2,1)} fusion(bf16[512,1792]{1,0:T(8,128)(2,1)S(1)} %fusion.3, bf16[1792,896]{1,0:T(8,128)(2,1)S(1)} %copy-done.14), kind=kOutput, calls=%fused_computation.22 | convolution fusion | flops 1644625920 | bytes 5963776 | tf_op jit(solution)/shard_map/dot_general | solution.py:206
  42.2 3.1 %reshape.169 = bf16[8,64,8,112]{3,2,1,0:T(8,128)(2,1)} reshape(bf16[512,896]{1,0:T(8,128)(2,1)} %convolution_convert_fusion.4) | data formatting | bytes 1835008 | tf_op jit(solution)/shard_map/reshape | solution.py:30
  45.3 0.1 iota_compare_fusion.6
  45.4 0.1 fusion.29
  45.5 0.8 broadcast_and_fusion
  46.3 36.3 %all-to-all-done.1 = bf16[8,32,2688]{2,1,0:T(8,128)(2,1)} async-done(((bf16[8,32,2688]{2,1,0:T(8,128)(2,1)}), bf16[8,32,2688]{2,1,0:T(8,128)(2,1)}, u32[]{:S(2)}, u32[]{:S(2)}) %all-to-all-start.1) | async-done | bytes 1376288 | tf_op jit(solution)/shard_map/all_to_all | solution.py:171
  82.6 2.1 convolution_convert_fusion
  84.7 0.1 slice.28
  84.8 0.0 copy-start.15
  84.8 0.6 convolution_convert_fusion.5
  85.5 0.4 multiply_convert_fusion
  85.9 0.8 copy-done.15
  86.7 3.0 fusion.6
  89.7 3.1 %reshape.168 = bf16[8,64,8,112]{3,2,1,0:T(8,128)(2,1)} reshape(bf16[512,896]{1,0:T(8,128)(2,1)} %fusion.6) | data formatting | bytes 1835008 | tf_op jit(solution)/shard_map/reshape | solution.py:29
  92.8 0.4 multiply_convert_fusion.1
  93.3 5.5 %fusion.7 = bf16[512,896]{1,0:T(8,128)(2,1)} fusion(bf16[512,896]{1,0:T(8,128)(2,1)S(1)} %bitcast.38, bf16[512,1792]{1,0:T(8,128)(2,1)} %copy-done.8, bf16[1792,896]{1,0:T(8,128)(2,1)} %param.19), kind=kOutput, calls=%fused_computation.18 | convolution fusion | flops 1645543424 | bytes 6881280 | tf_op jit(solution)/shard_map/dot_general | solution.py:208
  98.8 3.2 %reshape.167 = bf16[8,64,8,112]{3,2,1,0:T(8,128)(2,1)} reshape(bf16[512,896]{1,0:T(8,128)(2,1)} %fusion.7) | data formatting | bytes 1835008 | tf_op jit(solution)/shard_map/reshape | solution.py:31
  101.9 4.2 %fusion.41 = (f32[8,8,64]{2,1,0:T(8,128)S(1)}, f32[8,8,64,64]{2,3,1,0:T(8,128)}) fusion(pred[8,64,64]{1,2,0:T(8,128)(4,1)S(1)} %copy-done.11, bf16[8,64,8,112]{3,2,1,0:T(8,128)(2,1)} %reshape.169, bf16[8,64,8,112]{3,2,1,0:T(8,128)(2,1)} %reshape.168), kind=kOutput, calls=%fused_computation.73 | convolution fusion | flops 60031040 | bytes 2932736 | tf_op jit(solution)/shard_map/sub | solution.py:45
  106.1 2.5 fusion.10
  108.6 1.7 copy.60
  110.3 2.7 reshape.170
  113.0 4.1 %fusion.4 = bf16[512,1792]{1,0:T(8,128)(2,1)S(1)} fusion(bf16[512,1792]{1,0:T(8,128)(2,1)} %param.15, bf16[512,896]{1,0:T(8,128)(2,1)} %reshape.170, bf16[896,1792]{1,0:T(8,128)(2,1)S(1)} %copy-done), kind=kOutput, calls=%fused_computation.9 | convolution fusion | flops 1646919680 | bytes 7798784 | tf_op jit(solution)/shard_map/dot_general | solution.py:214
  117.1 0.0 copy-start.18
  117.1 2.4 convolution_convert_fusion.2
  119.6 4.2 %all-to-all-start.2 = ((bf16[32,16,1792]{2,1,0:T(8,128)(2,1)}), bf16[32,16,1792]{2,1,0:T(8,128)(2,1)S(1)}, u32[]{:S(2)}, u32[]{:S(2)}) async-start(bf16[32,16,1792]{2,1,0:T(8,128)(2,1)} %bitcast.37), calls=%async_computation.2 | async-start | bytes 3670016 | tf_op jit(solution)/shard_map/all_to_all | solution.py:220
  123.8 50.9 %all-to-all-done.2 = bf16[32,16,1792]{2,1,0:T(8,128)(2,1)S(1)} async-done(((bf16[32,16,1792]{2,1,0:T(8,128)(2,1)}), bf16[32,16,1792]{2,1,0:T(8,128)(2,1)S(1)}, u32[]{:S(2)}, u32[]{:S(2)}) %all-to-all-start.2) | async-done | bytes 1835040 | tf_op jit(solution)/shard_map/all_to_all | solution.py:220
  174.7 12.1 %gate_units.1 = (bf16[512,1792]{1,0:T(8,128)(2,1)S(1)}, f32[512,3584]{1,0:T(8,128)S(1)}) custom-call(bf16[512,1792]{1,0:T(8,128)(2,1)S(1)} %bitcast.35, f32[1,1792]{1,0:T(1,128)S(1)} %broadcast_in_dim.35.gain_ref, bf16[1792,3584]{1,0:T(8,128)(2,1)} %all-gather.4.cloned.1.call-done.w_ref), custom_call_target="tpu_custom_call" | custom-call | tf_op jit(solution)/shard_map/gate_units/pallas_call | solution.py:78
  186.8 2.9 copy-done.2
  189.8 1.3 copy-done.3
  191.1 32.5 %all-gather.8.cloned.1.call-done.w_ref = bf16[1792,2560]{1,0:T(8,128)(2,1)} async-done(((bf16[56,2560]{1,0:T(8,128)(2,1)}), bf16[1792,2560]{1,0:T(8,128)(2,1)}) %all-gather.8.cloned.1.call-update) | async-done | bytes 9175056 | tf_op jit(solution)/shard_map/all_gather | solution.py:148
  223.6 1.5 copy-done.4
  225.1 10.1 %up_units.2.refs_0_ = bf16[512,3584]{1,0:T(8,128)(2,1)} custom-call(bf16[512,1792]{1,0:T(8,128)(2,1)S(1)} %copy-done.4, f32[512,3584]{1,0:T(8,128)} %copy-done.2, bf16[1792,2560]{1,0:T(8,128)(2,1)} %all-gather.8.cloned.1.call-done.w_ref), custom_call_target="tpu_custom_call" | custom-call | tf_op jit(solution)/shard_map/up_units/pallas_call | solution.py:106
  235.2 50.5 %all-gather.6.cloned.1.call-done.w_ref = bf16[1792,1024]{1,0:T(8,128)(2,1)} async-done(((bf16[56,1024]{1,0:T(8,128)(2,1)}), bf16[1792,1024]{1,0:T(8,128)(2,1)}) %all-gather.6.cloned.1.call-update) | async-done | bytes 3670032 | tf_op jit(solution)/shard_map/all_gather | solution.py:149
  285.7 1.5 copy-done.5
  287.2 2.0 copy-done.6
  289.2 4.4 %up_units.3 = bf16[512,3584]{1,0:T(8,128)(2,1)} custom-call(bf16[512,1792]{1,0:T(8,128)(2,1)S(1)} %copy-done.5, f32[512,3584]{1,0:T(8,128)} %copy-done.2, bf16[1792,1024]{1,0:T(8,128)(2,1)S(1)} %copy-done.6, bf16[512,3584]{1,0:T(8,128)(2,1)} %up_units.2.refs_0_), custom_call_target="tpu_custom_call", output_to_operand_aliasing={{}: (3, {})} | custom-call | tf_op jit(solution)/shard_map/up_units/pallas_call | solution.py:106
  (29 shorter events, 0.1 us)
Async XLA Ops:
  7.2 105.9 %copy-start = (bf16[896,1792]{1,0:T(8,128)(2,1)S(1)}, bf16[896,1792]{1,0:T(8,128)(2,1)}, u32[]{:S(2)}) copy-start(bf16[896,1792]{1,0:T(8,128)(2,1)} %param.20) | copy-start | bytes 9633796
  7.2 13.9 %copy-start.10 = (bf16[4,2,16,896]{3,2,1,0:T(8,128)(2,1)S(1)}, bf16[4,2,16,896]{3,2,1,0:T(8,128)(2,1)}, u32[]{:S(2)}) copy-start(bf16[4,2,16,896]{3,2,1,0:T(8,128)(2,1)} %param.25) | copy-start | bytes 688132
  7.2 167.5 %all-gather.4.cloned.1.call-start = ((), (), s32[]{:S(2)}) async-start(), calls=%async_computation.3 | async-start | bytes 13246464 | tf_op jit(solution)/shard_map/all_gather | solution.py:146
  7.9 215.7 %all-gather.8.cloned.1.call-start = ((), (), s32[]{:S(2)}) async-start(), calls=%async_computation.5 | async-start | bytes 9461760 | tf_op jit(solution)/shard_map/all_gather | solution.py:148
  11.6 13.7 %all-to-all-start = ((bf16[8,1,4]{2,1,0:T(2,128)(2,1)}), bf16[8,1,4]{2,1,0:T(2,128)(2,1)S(1)}, u32[]{:S(2)}, u32[]{:S(2)}) async-start(bf16[8,1,4]{2,1,0:T(2,128)(2,1)} %copy.47), calls=%async_computation | async-start | bytes 8192 | tf_op jit(solution)/shard_map/all_to_all | solution.py:160
  28.4 8.1 %copy-start.12 = (f32[1792]{0:T(1024)S(1)}, f32[1792]{0:T(1024)}, u32[]{:S(2)}) copy-start(f32[1792]{0:T(1024)} %param.16) | copy-start | bytes 21508
  28.4 54.2 %all-to-all-start.1 = ((bf16[8,32,2688]{2,1,0:T(8,128)(2,1)}), bf16[8,32,2688]{2,1,0:T(8,128)(2,1)}, u32[]{:S(2)}, u32[]{:S(2)}) async-start(bf16[8,32,2688]{2,1,0:T(8,128)(2,1)} %copy.51), calls=%async_computation.1 | async-start | bytes 2752512 | tf_op jit(solution)/shard_map/all_to_all | solution.py:171
  32.8 252.8 %all-gather.6.cloned.1.call-start = ((), (), s32[]{:S(2)}) async-start(), calls=%async_computation.4 | async-start | bytes 3784704 | tf_op jit(solution)/shard_map/all_gather | solution.py:149
  34.5 2.1 copy-start.7
  36.6 2.6 copy-start.14
  37.1 1.2 copy-start.8
  42.2 3.2 %copy-start.17 = (s32[8]{0:T(128)S(1)}, s32[8]{0:T(128)}, u32[]{:S(2)}) copy-start(s32[8]{0:T(128)} %param.21) | copy-start | bytes 100
  82.6 2.2 copy-start.9
  84.8 1.9 copy-start.15
  98.8 3.2 %copy-start.11 = (pred[8,64,64]{1,2,0:T(8,128)(4,1)S(1)}, pred[8,64,64]{1,2,0:T(8,128)(4,1)}, u32[]{:S(2)}) copy-start(pred[8,64,64]{1,2,0:T(8,128)(4,1)} %broadcast_and_fusion) | copy-start | bytes 98308
  113.0 4.1 %copy-start.16 = (s32[1,512]{1,0:T(1,128)S(1)}, s32[1,512]{1,0:T(1,128)}, u32[]{:S(2)}) copy-start(s32[1,512]{1,0:T(1,128)} %param.26) | copy-start | bytes 6148
  117.1 2.4 copy-start.18
  119.6 4.2 %copy-start.13 = (f32[1792]{0:T(1024)S(1)}, f32[1792]{0:T(1024)}, u32[]{:S(2)}) copy-start(f32[1792]{0:T(1024)} %param.27) | copy-start | bytes 21508
  119.6 55.2 %all-to-all-start.2 = ((bf16[32,16,1792]{2,1,0:T(8,128)(2,1)}), bf16[32,16,1792]{2,1,0:T(8,128)(2,1)S(1)}, u32[]{:S(2)}, u32[]{:S(2)}) async-start(bf16[32,16,1792]{2,1,0:T(8,128)(2,1)} %bitcast.37), calls=%async_computation.2 | async-start | bytes 3670016 | tf_op jit(solution)/shard_map/all_to_all | solution.py:220
  186.8 2.9 copy-start.2
  189.8 1.3 copy-start.3
  223.6 1.5 copy-start.4
  285.7 1.5 copy-start.5
  287.2 2.0 copy-start.6
  289.2 4.4 %copy-start.1 = (bf16[896,1792]{1,0:T(8,128)(2,1)S(1)}, bf16[896,1792]{1,0:T(8,128)(2,1)}, u32[]{:S(2)}) copy-start(bf16[896,1792]{1,0:T(8,128)(2,1)} %param.20) | copy-start | bytes 9633796
Sparse Core Ops, SparseCore 0:
  10.9 119.7 all-gather.3
  133.6 89.9 all-gather.7
  226.5 59.1 all-gather.5
